TPU v7x, 1024 devices: a whole 4x4x32 slice. The times are simulated.
1024 devices in a mesh: expert: 64 (over x, z_lo, core), tensor: 16 (over z_hi, y).
Axes of the slice: x: 4, y: 4, z: 32 (z_hi: 4, z_lo: 8; z = z_hi * 8 + z_lo), core: 2. Of those that a mesh axis runs over, the one named last changes fastest.
Arguments:
- tokens: bfloat16 [8192, 2560], P(('expert', 'tensor')), may hold values from -12 to 12
- expert_ids: int32 [8192], P(('expert', 'tensor')), may hold values from 0 to 63, as said below
- slot_ids: int32 [8192], P(('expert', 'tensor')), may hold values from 0 to 3
- router: bfloat16 [2560, 64], replicated, may hold values from -0.125 to 0.125
- w_gate: bfloat16 [64, 2560, 4096], P('expert', None, 'tensor'), may hold values from -0.125 to 0.125
- w_up: bfloat16 [64, 2560, 4096], P('expert', None, 'tensor'), may hold values from -0.125 to 0.125
- hidden_grad: bfloat16 [64, 256, 4096], P('expert', None, 'tensor'), may hold values from -6 to 6
Outputs:
- activation: bfloat16 [64, 256, 4096], P('expert', None, 'tensor')
- token_grad: bfloat16 [8192, 2560], P(('expert', 'tensor'))
Inputs may be any that keep to these rules, and one draw needn't show every extreme that they name: expert_ids and slot_ids are drawn together. Within each aligned group of 128 consecutive tokens no two tokens share both expert and slot, so a group sends at most 4 tokens to one expert; in every draw one expert takes all 4 slots of every group.
All inputs are finite; a program needn't handle non-finite values.
Results may differ from a plain program's by a relative error of at most 0.02.
Values may be sent and summed in bfloat16 or wider, within the bound.
No kernel may reach another device: no remote copies, remote signals or barrier semaphores. Data moves between devices by JAX's collectives and lax.ppermute only.
A program may use at most 32 MiB of HBM per device.

v0:
```python
import jax
import jax.numpy as jnp
from jax import lax
from jax.sharding import PartitionSpec as P


def route_slots(buffer):
    return lax.all_to_all(buffer, "expert", split_axis=0, concat_axis=0, tiled=True)


def shards(tokens, expert_ids, slot_ids, router, w_gate, w_up, hidden_grad):
    n_tensor = lax.axis_size("tensor")
    n_expert = lax.axis_size("expert")
    tok_rows, feature_width = tokens.shape
    experts_all = router.shape[1]
    rows_all = hidden_grad.shape[1]
    capacity = rows_all // n_expert
    piece_width = feature_width // n_tensor
    gate_weight = w_gate[0]
    up_weight = w_up[0]
    logits = jnp.dot(tokens, router, preferred_element_type=jnp.float32)
    picked_mask = expert_ids[:, None] == jnp.arange(experts_all, dtype=jnp.int32)[None, :]
    picked = jnp.sum(jnp.where(picked_mask, logits, 0.0), axis=1)
    router_score = jax.nn.sigmoid(picked)
    routed_in = (router_score[:, None] * tokens.astype(jnp.float32)).astype(jnp.bfloat16)
    routing = jnp.stack([expert_ids, slot_ids], axis=1)
    group_rows, group_routing = (
        lax.all_gather(routed_in, "tensor", axis=0, tiled=True),
        lax.all_gather(routing, "tensor", axis=0, tiled=True),
    )
    target_row = group_routing[:, 0] * capacity + group_routing[:, 1]
    outgoing = (
        jnp.zeros((experts_all * capacity, feature_width), jnp.bfloat16)
        .at[target_row]
        .set(group_rows)
    )
    arrived = lax.all_to_all(
        outgoing.reshape(experts_all, capacity, feature_width),
        "expert",
        split_axis=0,
        concat_axis=0,
        tiled=True,
    )
    arrived = arrived.reshape(rows_all, feature_width)
    gate_proj = jnp.dot(arrived, gate_weight, preferred_element_type=jnp.float32)
    lifted = jnp.dot(arrived, up_weight, preferred_element_type=jnp.float32)
    sigma_gate = jax.nn.sigmoid(gate_proj)
    silu_gate = gate_proj * sigma_gate
    silu_slope = sigma_gate * (1.0 + gate_proj * (1.0 - sigma_gate))
    activation = (silu_gate * lifted).astype(jnp.bfloat16)
    cotangent = hidden_grad[0].astype(jnp.float32)
    d_gate = (cotangent * lifted * silu_slope).astype(jnp.bfloat16)
    d_lifted = (cotangent * silu_gate).astype(jnp.bfloat16)
    contract = (((1,), (1,)), ((), ()))
    partial_value = lax.dot_general(
        d_gate, gate_weight, contract, preferred_element_type=jnp.float32
    )
    partial_value = partial_value + lax.dot_general(
        d_lifted, up_weight, contract, preferred_element_type=jnp.float32
    )
    summed = lax.psum_scatter(
        partial_value.astype(jnp.bfloat16), "tensor", scatter_dimension=1, tiled=True
    )
    returned = route_slots(summed.reshape(n_expert, capacity, piece_width)).reshape(
        experts_all * capacity, piece_width
    )
    mine_rows = returned[target_row]
    ordered = mine_rows.reshape(n_tensor, tok_rows, piece_width).transpose(1, 0, 2)
    returned_rows = lax.all_to_all(ordered, "tensor", split_axis=1, concat_axis=1, tiled=True)
    d_float = returned_rows.reshape(tok_rows, feature_width).astype(jnp.float32)
    inner = jnp.sum(tokens.astype(jnp.float32) * d_float, axis=1)
    router_column = lax.dot_general(
        picked_mask.astype(jnp.bfloat16), router, contract, preferred_element_type=jnp.float32
    )
    gradient = (
        router_score[:, None] * d_float
        + (inner * router_score * (1.0 - router_score))[:, None] * router_column
    )
    return (activation[None], gradient.astype(jnp.bfloat16))


def solution(mesh):
    in_specs = (
        P(("expert", "tensor"), None),
        P(("expert", "tensor")),
        P(("expert", "tensor")),
        P(),
        P("expert", None, "tensor"),
        P("expert", None, "tensor"),
        P("expert", None, "tensor"),
    )
    out_specs = (P("expert", None, "tensor"), P(("expert", "tensor"), None))
    return jax.shard_map(shards, mesh=mesh, in_specs=in_specs, out_specs=out_specs, check_vma=False)
```

profile of v0, /device:TPU:32, one launch (start us, length us, event | category | flops | bytes accessed | tf_op | source)
XLA Modules:
  0.0 520.9 jit_solution(10507661947411925294)
XLA Ops:
  7.2 0.0 copy-start
  7.2 0.0 reduce-scatter.2.cloned.1.call-start
  7.2 0.8 add_bitcast_fusion
  8.0 87.1 %all-gather = s32[16,8,2]{1,2,0:T(2,128)S(1)} all-gather(s32[1,8,2]{1,2,0:T(2,128)S(1)} %add_bitcast_fusion), channel_id=1, replica_groups=mesh['expert'=64,'tensor'=16] {'tensor'}, dimensions={0}, use_global_device_ids=true | all-gather | bytes 1088 | tf_op jit(solution)/shard_map/all_gather | solution.py:29
  95.1 0.1 reshape.62
  95.2 1.3 fusion.10
  96.5 0.9 fusion.23
  97.3 86.5 %all_gather.7 = bf16[128,2560]{1,0:T(8,128)(2,1)S(1)} all-gather(bf16[8,2560]{1,0:T(8,128)(2,1)S(1)} %fusion.23), channel_id=1, replica_groups=mesh['expert'=64,'tensor'=16] {'tensor'}, dimensions={0}, use_global_device_ids=true | all-gather | bytes 696320 | tf_op jit(solution)/shard_map/all_gather | solution.py:28
  183.8 2.0 scatter_custom_fusion
  185.8 1.2 reshape.38
  187.0 67.2 %all_to_all.15 = bf16[64,4,2560]{2,1,0:T(4,128)(2,1)} all-to-all(bf16[64,4,2560]{2,1,0:T(4,128)(2,1)} %reshape.38), channel_id=1, replica_groups=mesh['expert'=64,'tensor'=16] {'expert'}, dimensions={0} | all-to-all | bytes 2621440 | tf_op jit(solution)/shard_map/all_to_all | solution.py:37
  254.3 2.5 reshape.39
  256.8 1.8 fusion.4
  258.6 0.0 copy-done
  258.6 0.0 copy-start.2
  258.6 0.5 fusion.8
  259.2 0.4 copy-done.2
  259.5 0.0 copy-start.1
  259.5 0.6 fusion.6
  260.1 0.7 copy-done.1
  260.9 1.6 fusion
  262.5 0.0 reduce-scatter.2.cloned.1.call-update
  262.5 181.0 %reduce-scatter.2.cloned.1.call-done = bf16[256,160]{0,1:T(8,128)(2,1)} async-done(((bf16[256,2560]{0,1:T(8,128)(2,1)}), bf16[256,160]{0,1:T(8,128)(2,1)}) %reduce-scatter.2.cloned.1.call-update) | async-done | bytes 81936 | tf_op jit(solution)/shard_map/reduce_scatter | solution.py:61
  443.5 1.0 copy.15
  444.5 0.0 copy-start.4
  444.5 0.0 copy-start.3
  444.5 0.0 copy-start.5
  444.5 0.7 reshape.40
  445.2 11.5 %all-to-all-start.1 = ((bf16[64,4,160]{2,1,0:T(4,128)(2,1)}), bf16[64,4,160]{2,1,0:T(4,128)(2,1)S(1)}, u32[]{:S(2)}, u32[]{:S(2)}) async-start(bf16[64,4,160]{2,1,0:T(4,128)(2,1)} %reshape.40), calls=%async_computation.2 | async-start | bytes 262144 | tf_op jit(solution)/shard_map/all_to_all | solution.py:8
  456.7 13.6 %all-to-all-done.1 = bf16[64,4,160]{2,1,0:T(4,128)(2,1)S(1)} async-done(((bf16[64,4,160]{2,1,0:T(4,128)(2,1)}), bf16[64,4,160]{2,1,0:T(4,128)(2,1)S(1)}, u32[]{:S(2)}, u32[]{:S(2)}) %all-to-all-start.1) | async-done | bytes 81952 | tf_op jit(solution)/shard_map/all_to_all | solution.py:8
  470.4 0.1 reshape.41
  470.5 1.5 gather_fusion
  471.9 13.5 %all-to-all-start.2 = ((bf16[8,16,160]{2,0,1:T(8,128)(2,1)}), bf16[8,16,160]{2,0,1:T(8,128)(2,1)S(1)}, u32[]{:S(2)}, u32[]{:S(2)}) async-start(bf16[8,16,160]{2,0,1:T(8,128)(2,1)} %bitcast.10), calls=%async_computation.3 | async-start | bytes 131072 | tf_op jit(solution)/shard_map/all_to_all | solution.py:69
  485.4 0.7 fusion.17
  486.1 26.8 %all-to-all-done.2 = bf16[8,16,160]{2,0,1:T(8,128)(2,1)S(1)} async-done(((bf16[8,16,160]{2,0,1:T(8,128)(2,1)}), bf16[8,16,160]{2,0,1:T(8,128)(2,1)S(1)}, u32[]{:S(2)}, u32[]{:S(2)}) %all-to-all-start.2) | async-done | bytes 40992 | tf_op jit(solution)/shard_map/all_to_all | solution.py:69
  513.0 0.1 reshape.44
  513.1 0.0 copy-done.4
  513.1 0.1 fusion.24
  513.2 0.0 copy-done.3
  513.2 0.0 copy-done.5
  513.3 0.8 fusion.2
  (6 shorter events, 0.0 us)
Async XLA Ops:
  7.2 251.5 %copy-start = (bf16[1,2560,256]{2,1,0:T(8,128)(2,1)S(1)}, bf16[1,2560,256]{2,1,0:T(8,128)(2,1)}, u32[]{:S(2)}) copy-start(bf16[1,2560,256]{2,1,0:T(8,128)(2,1)} %param.11) | copy-start | bytes 3932164
  7.2 436.3 %reduce-scatter.2.cloned.1.call-start = ((), (), s32[]{:S(2)}) async-start(), calls=%async_computation.4 | async-start | bytes 1392640 | tf_op jit(solution)/shard_map/reduce_scatter | solution.py:61
  258.6 0.9 copy-start.2
  259.5 1.3 copy-start.1
  444.5 68.6 %copy-start.4 = (bf16[8,2560]{1,0:T(8,128)(2,1)S(1)}, bf16[8,2560]{1,0:T(8,128)(2,1)}, u32[]{:S(2)}) copy-start(bf16[8,2560]{1,0:T(8,128)(2,1)} %param.7) | copy-start | bytes 122884
  444.5 68.7 %copy-start.3 = (bf16[2560,64]{0,1:T(8,128)(2,1)S(1)}, bf16[2560,64]{0,1:T(8,128)(2,1)}, u32[]{:S(2)}) copy-start(bf16[2560,64]{0,1:T(8,128)(2,1)} %param.10) | copy-start | bytes 983044
  444.5 68.7 %copy-start.5 = (s32[8]{0:T(128)S(1)}, s32[8]{0:T(128)}, u32[]{:S(2)}) copy-start(s32[8]{0:T(128)} %param.8) | copy-start | bytes 100
  445.2 25.1 %all-to-all-start.1 = ((bf16[64,4,160]{2,1,0:T(4,128)(2,1)}), bf16[64,4,160]{2,1,0:T(4,128)(2,1)S(1)}, u32[]{:S(2)}, u32[]{:S(2)}) async-start(bf16[64,4,160]{2,1,0:T(4,128)(2,1)} %reshape.40), calls=%async_computation.2 | async-start | bytes 262144 | tf_op jit(solution)/shard_map/all_to_all | solution.py:8
  471.9 41.0 %all-to-all-start.2 = ((bf16[8,16,160]{2,0,1:T(8,128)(2,1)}), bf16[8,16,160]{2,0,1:T(8,128)(2,1)S(1)}, u32[]{:S(2)}, u32[]{:S(2)}) async-start(bf16[8,16,160]{2,0,1:T(8,128)(2,1)} %bitcast.10), calls=%async_computation.3 | async-start | bytes 131072 | tf_op jit(solution)/shard_map/all_to_all | solution.py:69
Sparse Core Ops, SparseCore 0:
  262.6 180.8 reduce-scatter.1
where the time goes:
time: 522 us; the launch traced here: 521 us
  blocking collectives  241 us (46%)
  waiting for transfers between devices  221 us (42%)
  starting transfers between devices  25 us (5%)
  between operations  14.2 us (3%)
  local copies, waits for them, and re-layouts  10.3 us (2%)
  matrix products  6.64 us (1%)
    reduce_scatter x1, waiting for transfers between devices, shards(): lax.psum_scatter(partial_value.astype(jnp.bfloat16), 'tensor', scatter_di...  181 us
    all_gather x1, blocking collectives, shards(): lax.all_gather(routing, 'tensor', axis=0, tiled=True)  87.1 us
    all_gather x1, blocking collectives, shards(): lax.all_gather(routed_in, 'tensor', axis=0, tiled=True)  86.5 us
    all_to_all x1, blocking collectives, shards(): lax.all_to_all(outgoing.reshape(experts_all, capacity, feature_width), 'e...  67.2 us
    all_to_all x1, waiting for transfers between devices, shards(): lax.all_to_all(ordered, 'tensor', split_axis=1, concat_axis=1, tiled=True)  26.8 us
    all_to_all x1, waiting for transfers between devices, route_slots(): lax.all_to_all(buffer, 'expert', split_axis=0, concat_axis=0, tiled=True)  13.6 us
    all_to_all x1, starting transfers between devices, shards(): lax.all_to_all(ordered, 'tensor', split_axis=1, concat_axis=1, tiled=True)  13.5 us
    all_to_all x1, starting transfers between devices, route_slots(): lax.all_to_all(buffer, 'expert', split_axis=0, concat_axis=0, tiled=True)  11.5 us
  transfers between devices with their start and end apart: 3, of which 3 were waited for; matrix products, arithmetic and copies ran while one was open for 0% of the time, Pallas kernels for 0%

commit v1 on v0

v1 whole, which is shorter than its diff:
```python
import math

import jax
import jax.numpy as jnp
from jax import lax
from jax.sharding import Mesh
from jax.sharding import PartitionSpec as P

CODE_COLUMNS = 128


def exchange(buffer, axes):
    return lax.all_to_all(buffer, axes, split_axis=0, concat_axis=0, tiled=True)


def shards(tokens, expert_ids, slot_ids, router, w_gate, w_up, hidden_grad):
    n_high, n_row, n_expert = lax.axis_size("high"), lax.axis_size("row"), lax.axis_size("expert")
    n_tensor = n_high * n_row
    tok_rows, width = tokens.shape
    experts_all = router.shape[1]
    rows_all = hidden_grad.shape[1]
    capacity = rows_all // n_expert
    piece = width // n_row
    group = n_tensor * tok_rows
    gate_weight, up_weight = w_gate[0], w_up[0]

    logits = jnp.dot(tokens, router, preferred_element_type=jnp.float32)
    picked_mask = expert_ids[:, None] == jnp.arange(experts_all, dtype=jnp.int32)[None, :]
    picked = jnp.sum(jnp.where(picked_mask, logits, 0.0), axis=1)
    router_score = jax.nn.sigmoid(picked)
    token_float = tokens.astype(jnp.float32)
    routed_in = (router_score[:, None] * token_float).astype(jnp.bfloat16)

    code = (expert_ids * capacity + slot_ids).astype(jnp.bfloat16)
    pieces = routed_in.reshape(tok_rows, n_row, piece).transpose(1, 0, 2)
    codes = jnp.broadcast_to(code[None, :, None], (n_row, tok_rows, CODE_COLUMNS))
    outgoing = jnp.concatenate([pieces, codes], axis=2)
    outgoing = jnp.broadcast_to(outgoing[None], (n_high,) + outgoing.shape)
    outgoing = outgoing.reshape(n_tensor, tok_rows, piece + CODE_COLUMNS)
    group_rows = exchange(outgoing, ("high", "row")).reshape(group, piece + CODE_COLUMNS)

    slot_numbers = jnp.arange(experts_all * capacity, dtype=jnp.int32)
    placed = group_rows[:, piece : piece + 1].astype(jnp.int32) == slot_numbers[None, :]
    placed = placed.astype(jnp.bfloat16)
    slots = lax.dot_general(
        placed, group_rows[:, :piece], (((0,), (0,)), ((), ())), preferred_element_type=jnp.float32
    ).astype(jnp.bfloat16)
    arrived = exchange(slots.reshape(experts_all, capacity, piece), "expert").reshape(rows_all, piece)
    arrived = exchange(jnp.broadcast_to(arrived[None], (n_row, rows_all, piece)), "row")

    gate_proj = jnp.zeros((rows_all, gate_weight.shape[1]), jnp.float32)
    lifted = gate_proj
    for y in range(n_row):
        cut = slice(y * piece, (y + 1) * piece)
        gate_proj += jnp.dot(arrived[y], gate_weight[cut], preferred_element_type=jnp.float32)
        lifted += jnp.dot(arrived[y], up_weight[cut], preferred_element_type=jnp.float32)
    sigma_gate = jax.nn.sigmoid(gate_proj)
    silu_gate = gate_proj * sigma_gate
    silu_slope = sigma_gate * (1.0 + gate_proj * (1.0 - sigma_gate))
    activation = (silu_gate * lifted).astype(jnp.bfloat16)
    cotangent = hidden_grad[0].astype(jnp.float32)
    d_gate = (cotangent * lifted * silu_slope).astype(jnp.bfloat16)
    d_lifted = (cotangent * silu_gate).astype(jnp.bfloat16)
    contract = (((1,), (1,)), ((), ()))
    partial = []
    for y in range(n_row):
        cut = slice(y * piece, (y + 1) * piece)
        part = lax.dot_general(d_gate, gate_weight[cut], contract, preferred_element_type=jnp.float32)
        part += lax.dot_general(d_lifted, up_weight[cut], contract, preferred_element_type=jnp.float32)
        partial.append(part.astype(jnp.bfloat16))

    partial = exchange(jnp.stack(partial), "row")
    summed = jnp.sum(partial.astype(jnp.float32), axis=0).astype(jnp.bfloat16)
    returned = exchange(summed.reshape(n_expert, capacity, piece), "expert").reshape(experts_all * capacity, piece)
    mine = jnp.dot(placed, returned, preferred_element_type=jnp.float32).astype(jnp.bfloat16)
    home = exchange(mine.reshape(n_tensor, tok_rows, piece), ("high", "row"))
    home = jnp.sum(home.reshape(n_high, n_row, tok_rows, piece).astype(jnp.float32), axis=0)
    d_float = home.transpose(1, 0, 2).reshape(tok_rows, width).astype(jnp.bfloat16).astype(jnp.float32)

    inner = jnp.sum(token_float * d_float, axis=1)
    router_column = lax.dot_general(
        picked_mask.astype(jnp.bfloat16), router, contract, preferred_element_type=jnp.float32
    )
    gradient = (
        router_score[:, None] * d_float
        + (inner * router_score * (1.0 - router_score))[:, None] * router_column
    )
    return activation[None], gradient.astype(jnp.bfloat16)


def solution(mesh):
    n_expert, n_tensor = mesh.devices.shape
    n_row = math.isqrt(n_tensor)
    split = Mesh(mesh.devices.reshape(n_expert, n_tensor // n_row, n_row), ("expert", "high", "row"))
    tensor = ("high", "row")
    owners = ("expert", "high", "row")
    in_specs = (
        P(owners, None),
        P(owners),
        P(owners),
        P(),
        P("expert", None, tensor),
        P("expert", None, tensor),
        P("expert", None, tensor),
    )
    out_specs = (P("expert", None, tensor), P(owners, None))
    return jax.shard_map(shards, mesh=split, in_specs=in_specs, out_specs=out_specs, check_vma=False)
```

time: 522 us -> 220 us (0.42)
  waiting for transfers between devices: 221 us -> 0 us
  blocking collectives: 241 us -> 206 us
  starting transfers between devices: 25 us -> 0 us
  between operations: 14.2 us -> 0.89 us
  local copies, waits for them, and re-layouts: 10.3 us -> 2.61 us
    reduce_scatter x1 -> x0, waiting for transfers between devices: 181 us -> none  [shards(): lax.psum_scatter(partial_value.astype(jnp.bfloat16), 'tensor', scatter_di...]
    all_gather x2 -> x0, blocking collectives: 174 us -> none  [the longest x1 87.1 us: shards(): lax.all_gather(routing, 'tensor', axis=0, tiled=True)]
    all_to_all x1 -> x6, blocking collectives: 67.2 us -> 206 us  [exchange(): return lax.all_to_all(buffer, axes, split_axis=0, concat_axis=0, tiled=True)]
    all_to_all x2 -> x0, waiting for transfers between devices: 40.5 us -> none  [the longest x1 26.8 us: shards(): lax.all_to_all(ordered, 'tensor', split_axis=1, concat_axis=1, tiled=True)]
    all_to_all x2 -> x0, starting transfers between devices: 24.9 us -> none  [the longest x1 13.5 us: shards(): lax.all_to_all(ordered, 'tensor', split_axis=1, concat_axis=1, tiled=True)]
  transfers between devices with their start and end apart: 3 -> 0, of which waited for: 3 -> 0; matrix products, arithmetic and copies ran while one was open for 0% -> 0% of each run, Pallas kernels for 0% -> 0%
where the time goes in v1:
time: 220 us
  blocking collectives  206 us (94%)
  matrix products  7.79 us (4%)
  local copies, waits for them, and re-layouts  2.61 us (1%)
  other arithmetic  2.37 us (1%)
    all_to_all x6, blocking collectives, exchange(): return lax.all_to_all(buffer, axes, split_axis=0, concat_axis=0, tiled=True)  206 us

profile of v1, /device:TPU:32, one launch (start us, length us, event | category | flops | bytes accessed | tf_op | source)
XLA Modules:
  0.0 219.9 jit_solution(16729711741159123656)
XLA Ops:
  0.6 0.0 copy-start
  0.6 1.0 copy-done
  1.6 1.1 fusion.11
  2.7 0.7 add_convert_fusion
  3.4 0.9 fusion.56
  4.3 0.1 broadcast_in_dim.15
  4.4 68.3 %all_to_all.30 = bf16[16,8,768]{2,1,0:T(8,128)(2,1)S(1)} all-to-all(bf16[16,8,768]{2,1,0:T(8,128)(2,1)S(1)} %bitcast.99), channel_id=1, replica_groups=mesh['expert'=64,'high'=4,'row'=4] {'high','row'}, dimensions={0} | all-to-all | bytes 393216 | tf_op jit(solution)/shard_map/all_to_all | solution.py:13
  72.7 0.1 convert_reduce_fusion
  72.8 0.4 convolution_convert_fusion
  73.2 0.1 reshape.62
  73.2 28.5 %all_to_all.31 = bf16[64,4,640]{2,1,0:T(4,128)(2,1)S(1)} all-to-all(bf16[64,4,640]{2,1,0:T(4,128)(2,1)S(1)} %reshape.62), channel_id=1, replica_groups=mesh['expert'=64,'high'=4,'row'=4] {'expert'}, dimensions={0} | all-to-all | bytes 655360 | tf_op jit(solution)/shard_map/all_to_all | solution.py:13
  101.8 0.1 broadcast_in_dim.17
  101.8 0.1 broadcast_in_dim.18
  101.9 0.0 copy-start.1
  102.0 20.8 %all_to_all.32 = bf16[4,256,640]{2,1,0:T(8,128)(2,1)S(1)} all-to-all(bf16[4,256,640]{2,1,0:T(8,128)(2,1)S(1)} %broadcast_in_dim.18), channel_id=1, replica_groups=mesh['expert'=64,'high'=4,'row'=4] {'row'}, dimensions={0} | all-to-all | bytes 2621440 | tf_op jit(solution)/shard_map/all_to_all | solution.py:13
  122.8 0.0 copy-done.1
  122.8 0.3 fusion.19
  123.1 0.3 convolution_add_fusion.6
  123.3 0.0 copy-start.2
  123.4 0.3 convolution_add_fusion.5
  123.6 0.3 convolution_add_fusion.4
  123.9 0.8 copy-done.2
  124.7 0.3 fusion.32
  124.9 0.0 copy-start.5
  125.0 0.3 convolution_add_fusion.9
  125.2 0.3 convolution_add_fusion.8
  125.5 0.3 copy-done.5
  125.8 1.0 fusion.51
  126.9 0.3 fusion.21
  127.2 0.3 fusion.24
  127.5 0.3 fusion.27
  127.8 0.3 fusion.30
  128.1 0.3 fusion.6
  128.4 0.3 fusion.7
  128.7 0.3 fusion.8
  129.0 0.3 fusion.9
  129.3 0.2 pad_maximum_fusion
  129.5 19.5 %all_to_all.33 = bf16[4,256,640]{2,1,0:T(8,128)(2,1)S(1)} all-to-all(bf16[4,256,640]{2,1,0:T(8,128)(2,1)S(1)} %pad_maximum_fusion), channel_id=1, replica_groups=mesh['expert'=64,'high'=4,'row'=4] {'row'}, dimensions={0} | all-to-all | bytes 2621440 | tf_op jit(solution)/shard_map/all_to_all | solution.py:13
  148.9 0.3 reduce_sum.40
  149.3 0.1 reshape.63
  149.4 0.0 copy-start.3
  149.4 0.0 copy-start.4
  149.4 29.1 %all_to_all.34 = bf16[64,4,640]{2,1,0:T(4,128)(2,1)S(1)} all-to-all(bf16[64,4,640]{2,1,0:T(4,128)(2,1)S(1)} %reshape.63), channel_id=1, replica_groups=mesh['expert'=64,'high'=4,'row'=4] {'expert'}, dimensions={0} | all-to-all | bytes 655360 | tf_op jit(solution)/shard_map/all_to_all | solution.py:13
  178.4 0.1 reshape.64
  178.5 0.2 fusion.10
  178.8 40.0 %all_to_all.35 = bf16[16,8,640]{2,1,0:T(8,128)(2,1)S(1)} all-to-all(bf16[16,8,640]{2,1,0:T(8,128)(2,1)S(1)} %fusion.10), channel_id=1, replica_groups=mesh['expert'=64,'high'=4,'row'=4] {'high','row'}, dimensions={0} | all-to-all | bytes 327680 | tf_op jit(solution)/shard_map/all_to_all | solution.py:13
  218.9 0.0 copy-done.3
  218.9 0.1 fusion.57
  219.0 0.0 copy-done.4
  219.0 0.8 fusion.1
  (6 shorter events, 0.1 us)
Async XLA Ops:
  0.6 1.0 copy-start
  101.9 20.9 %copy-start.1 = (bf16[1,2560,256]{2,1,0:T(8,128)(2,1)S(1)}, bf16[1,2560,256]{2,1,0:T(8,128)(2,1)}, u32[]{:S(2)}) copy-start(bf16[1,2560,256]{2,1,0:T(8,128)(2,1)} %param.12) | copy-start | bytes 3932164
  123.3 1.3 copy-start.2
  124.9 0.9 copy-start.5
  149.4 69.5 %copy-start.3 = (bf16[8,2560]{1,0:T(8,128)(2,1)S(1)}, bf16[8,2560]{1,0:T(8,128)(2,1)}, u32[]{:S(2)}) copy-start(bf16[8,2560]{1,0:T(8,128)(2,1)} %param.7) | copy-start | bytes 122884
  149.4 69.7 %copy-start.4 = (s32[8]{0:T(128)S(1)}, s32[8]{0:T(128)}, u32[]{:S(2)}) copy-start(s32[8]{0:T(128)} %param.8) | copy-start | bytes 100

commit v2 on v1

--- a/solution.py
+++ b/solution.py
@@ -13,9 +13,16 @@
     return lax.all_to_all(buffer, axes, split_axis=0, concat_axis=0, tiled=True)
 
 
+def swap_rows(rows, outer, inner, unit):
+    out = lax.broadcasted_iota(jnp.int32, (rows, rows), 0)
+    source = (out // unit % inner * outer + out // (unit * inner)) * unit + out % unit
+    return (source == lax.broadcasted_iota(jnp.int32, (rows, rows), 1)).astype(jnp.bfloat16)
+
+
 def shards(tokens, expert_ids, slot_ids, router, w_gate, w_up, hidden_grad):
-    n_high, n_row, n_expert = lax.axis_size("high"), lax.axis_size("row"), lax.axis_size("expert")
-    n_tensor = n_high * n_row
+    n_high, n_row = lax.axis_size("high"), lax.axis_size("row")
+    n_x, n_pair = lax.axis_size("x"), lax.axis_size("pair")
+    n_tensor, n_expert = n_high * n_row, n_x * n_pair
     tok_rows, width = tokens.shape
     experts_all = router.shape[1]
     rows_all = hidden_grad.shape[1]
@@ -31,7 +38,7 @@
     token_float = tokens.astype(jnp.float32)
     routed_in = (router_score[:, None] * token_float).astype(jnp.bfloat16)
 
-    code = (expert_ids * capacity + slot_ids).astype(jnp.bfloat16)
+    code = ((expert_ids % n_pair * n_x + expert_ids // n_pair) * capacity + slot_ids).astype(jnp.bfloat16)
     pieces = routed_in.reshape(tok_rows, n_row, piece).transpose(1, 0, 2)
     codes = jnp.broadcast_to(code[None, :, None], (n_row, tok_rows, CODE_COLUMNS))
     outgoing = jnp.concatenate([pieces, codes], axis=2)
@@ -45,8 +52,13 @@
     slots = lax.dot_general(
         placed, group_rows[:, :piece], (((0,), (0,)), ((), ())), preferred_element_type=jnp.float32
     ).astype(jnp.bfloat16)
-    arrived = exchange(slots.reshape(experts_all, capacity, piece), "expert").reshape(rows_all, piece)
-    arrived = exchange(jnp.broadcast_to(arrived[None], (n_row, rows_all, piece)), "row")
+    planes = exchange(slots.reshape(n_pair, n_x * capacity, piece), "pair").reshape(rows_all, piece)
+    x_first = swap_rows(rows_all, n_x, n_pair, capacity)
+    planes = jnp.dot(x_first, planes, preferred_element_type=jnp.float32).astype(jnp.bfloat16)
+    block = n_pair * capacity
+    planes = jnp.broadcast_to(planes.reshape(1, n_x, block, piece), (n_row, n_x, block, piece))
+    arrived = exchange(planes.reshape(n_row * n_x, block, piece), ("row", "x"))
+    arrived = arrived.reshape(n_row, rows_all, piece)
 
     gate_proj = jnp.zeros((rows_all, gate_weight.shape[1]), jnp.float32)
     lifted = gate_proj
@@ -69,9 +81,11 @@
         part += lax.dot_general(d_lifted, up_weight[cut], contract, preferred_element_type=jnp.float32)
         partial.append(part.astype(jnp.bfloat16))
 
-    partial = exchange(jnp.stack(partial), "row")
-    summed = jnp.sum(partial.astype(jnp.float32), axis=0).astype(jnp.bfloat16)
-    returned = exchange(summed.reshape(n_expert, capacity, piece), "expert").reshape(experts_all * capacity, piece)
+    partial = exchange(jnp.stack(partial).reshape(n_row * n_x, block, piece), ("row", "x"))
+    summed = jnp.sum(partial.reshape(n_row, rows_all, piece).astype(jnp.float32), axis=0).astype(jnp.bfloat16)
+    pair_first = swap_rows(rows_all, n_pair, n_x, capacity)
+    summed = jnp.dot(pair_first, summed, preferred_element_type=jnp.float32).astype(jnp.bfloat16)
+    returned = exchange(summed.reshape(n_pair, n_x * capacity, piece), "pair").reshape(experts_all * capacity, piece)
     mine = jnp.dot(placed, returned, preferred_element_type=jnp.float32).astype(jnp.bfloat16)
     home = exchange(mine.reshape(n_tensor, tok_rows, piece), ("high", "row"))
     home = jnp.sum(home.reshape(n_high, n_row, tok_rows, piece).astype(jnp.float32), axis=0)
@@ -90,18 +104,18 @@
 
 def solution(mesh):
     n_expert, n_tensor = mesh.devices.shape
-    n_row = math.isqrt(n_tensor)
-    split = Mesh(mesh.devices.reshape(n_expert, n_tensor // n_row, n_row), ("expert", "high", "row"))
-    tensor = ("high", "row")
-    owners = ("expert", "high", "row")
+    n_row = n_x = math.isqrt(n_tensor)
+    axes = ("x", "pair", "high", "row")
+    split = Mesh(mesh.devices.reshape(n_x, n_expert // n_x, n_tensor // n_row, n_row), axes)
+    expert, tensor = axes[:2], axes[2:]
     in_specs = (
-        P(owners, None),
-        P(owners),
-        P(owners),
+        P(axes, None),
+        P(axes),
+        P(axes),
         P(),
-        P("expert", None, tensor),
-        P("expert", None, tensor),
-        P("expert", None, tensor),
+        P(expert, None, tensor),
+        P(expert, None, tensor),
+        P(expert, None, tensor),
     )
-    out_specs = (P("expert", None, tensor), P(owners, None))
+    out_specs = (P(expert, None, tensor), P(axes, None))
     return jax.shard_map(shards, mesh=split, in_specs=in_specs, out_specs=out_specs, check_vma=False)

time: 220 us -> 222 us (level)
  the two profiles are of different devices: /device:TPU:32 before, /device:TPU:57 now
where the time goes in v2:
time: 222 us; the launch traced here: 221 us
  blocking collectives  153 us (69%)
  waiting for transfers between devices  35.9 us (16%)
  starting transfers between devices  14.9 us (7%)
  matrix products  10.4 us (5%)
  other arithmetic  3.38 us (2%)
  local copies, waits for them, and re-layouts  2.29 us (1%)
    all_to_all x4, blocking collectives, exchange(): return lax.all_to_all(buffer, axes, split_axis=0, concat_axis=0, tiled=True)  153 us
    all_to_all x2, waiting for transfers between devices, exchange(): return lax.all_to_all(buffer, axes, split_axis=0, concat_axis=0, tiled=True)  35.9 us
    all_to_all x2, starting transfers between devices, exchange(): return lax.all_to_all(buffer, axes, split_axis=0, concat_axis=0, tiled=True)  14.9 us
  transfers between devices with their start and end apart: 2, of which 2 were waited for; matrix products, arithmetic and copies ran while one was open for 0% of the time, Pallas kernels for 0%

profile of v2, /device:TPU:57, one launch (start us, length us, event | category | flops | bytes accessed | tf_op | source)
XLA Modules:
  0.0 221.0 jit_solution(14255004642031074404)
XLA Ops:
  0.6 0.0 copy-start
  0.6 0.7 add_convert_fusion
  1.4 0.3 copy-done
  1.6 1.1 fusion.11
  2.7 0.9 fusion.100
  3.6 0.1 broadcast_in_dim.15
  3.7 63.3 %all_to_all.30 = bf16[16,8,768]{2,1,0:T(8,128)(2,1)S(1)} all-to-all(bf16[16,8,768]{2,1,0:T(8,128)(2,1)S(1)} %bitcast.116), channel_id=1, replica_groups=mesh['x'=4,'pair'=16,'high'=4,'row'=4] {'high','row'}, dimensions={0} | all-to-all | bytes 393216 | tf_op jit(solution)/shard_map/all_to_all | solution.py:13
  67.0 0.1 convert_reduce_fusion
  67.1 1.1 convolution_convert_fusion.2
  68.2 9.2 %all-to-all-start.1 = ((bf16[16,16,640]{2,1,0:T(8,128)(2,1)}), bf16[16,16,640]{2,1,0:T(8,128)(2,1)S(1)}, u32[]{:S(2)}, u32[]{:S(2)}) async-start(bf16[16,16,640]{2,1,0:T(8,128)(2,1)} %bitcast.4), calls=%async_computation.1 | async-start | bytes 655360 | tf_op jit(solution)/shard_map/all_to_all | solution.py:13
  77.4 18.7 %all-to-all-done.1 = bf16[16,16,640]{2,1,0:T(8,128)(2,1)S(1)} async-done(((bf16[16,16,640]{2,1,0:T(8,128)(2,1)}), bf16[16,16,640]{2,1,0:T(8,128)(2,1)S(1)}, u32[]{:S(2)}, u32[]{:S(2)}) %all-to-all-start.1) | async-done | bytes 327712 | tf_op jit(solution)/shard_map/all_to_all | solution.py:13
  96.1 0.9 convolution_convert_fusion.1
  97.0 0.1 broadcast_in_dim.18
  97.1 24.8 %all_to_all.31 = bf16[16,64,640]{2,1,0:T(8,128)(2,1)S(1)} all-to-all(bf16[16,64,640]{2,1,0:T(8,128)(2,1)S(1)} %bitcast.104), channel_id=1, replica_groups=mesh['x'=4,'pair'=16,'high'=4,'row'=4] {'row','x'}, dimensions={0} | all-to-all | bytes 2621440 | tf_op jit(solution)/shard_map/all_to_all | solution.py:13
  122.0 0.0 copy-start.1
  122.0 0.0 copy-start.2
  122.0 0.1 fusion.119
  122.1 1.2 copy-done.1
  123.3 0.3 fusion.19
  123.6 0.1 copy-done.2
  123.7 0.3 fusion.32
  124.0 0.3 convolution_add_fusion.6
  124.3 0.3 convolution_add_fusion.9
  124.5 0.3 convolution_add_fusion.5
  124.8 0.0 copy-start.5
  124.8 0.3 convolution_add_fusion.8
  125.1 0.3 convolution_add_fusion.4
  125.4 0.3 copy-done.5
  125.7 1.0 fusion.51
  126.7 0.3 fusion.21
  127.0 0.3 fusion.24
  127.3 0.3 fusion.27
  127.6 0.3 fusion.30
  127.9 0.3 fusion.6
  128.2 0.3 fusion.7
  128.5 0.3 fusion.8
  128.9 0.3 fusion.9
  129.2 1.3 pad_maximum_fusion
  130.4 5.7 %all-to-all-start.3 = ((bf16[16,64,640]{2,1,0:T(8,128)(2,1)}), bf16[16,64,640]{2,1,0:T(8,128)(2,1)S(1)}, u32[]{:S(2)}, u32[]{:S(2)}) async-start(bf16[16,64,640]{2,1,0:T(8,128)(2,1)} %bitcast.27), calls=%async_computation.3 | async-start | bytes 2621440 | tf_op jit(solution)/shard_map/all_to_all | solution.py:13
  136.1 17.2 %all-to-all-done.3 = bf16[16,64,640]{2,1,0:T(8,128)(2,1)S(1)} async-done(((bf16[16,64,640]{2,1,0:T(8,128)(2,1)}), bf16[16,64,640]{2,1,0:T(8,128)(2,1)S(1)}, u32[]{:S(2)}, u32[]{:S(2)}) %all-to-all-start.3) | async-done | bytes 1310752 | tf_op jit(solution)/shard_map/all_to_all | solution.py:13
  153.4 0.2 bitcast_reduce_fusion
  153.5 0.9 convolution_convert_fusion
  154.5 0.0 copy-start.3
  154.5 0.0 copy-start.4
  154.5 26.0 %all_to_all.32 = bf16[16,16,640]{2,1,0:T(8,128)(2,1)S(1)} all-to-all(bf16[16,16,640]{2,1,0:T(8,128)(2,1)S(1)} %bitcast.121), channel_id=1, replica_groups=mesh['x'=4,'pair'=16,'high'=4,'row'=4] {'pair'}, dimensions={0} | all-to-all | bytes 655360 | tf_op jit(solution)/shard_map/all_to_all | solution.py:13
  180.5 0.2 fusion.10
  180.7 39.2 %all_to_all.33 = bf16[16,8,640]{2,1,0:T(8,128)(2,1)S(1)} all-to-all(bf16[16,8,640]{2,1,0:T(8,128)(2,1)S(1)} %fusion.10), channel_id=1, replica_groups=mesh['x'=4,'pair'=16,'high'=4,'row'=4] {'high','row'}, dimensions={0} | all-to-all | bytes 327680 | tf_op jit(solution)/shard_map/all_to_all | solution.py:13
  220.0 0.0 copy-done.3
  220.0 0.1 fusion.101
  220.2 0.0 copy-done.4
  220.2 0.8 fusion.1
  (13 shorter events, 0.1 us)
Async XLA Ops:
  0.6 1.0 copy-start
  68.2 27.9 %all-to-all-start.1 = ((bf16[16,16,640]{2,1,0:T(8,128)(2,1)}), bf16[16,16,640]{2,1,0:T(8,128)(2,1)S(1)}, u32[]{:S(2)}, u32[]{:S(2)}) async-start(bf16[16,16,640]{2,1,0:T(8,128)(2,1)} %bitcast.4), calls=%async_computation.1 | async-start | bytes 655360 | tf_op jit(solution)/shard_map/all_to_all | solution.py:13
  122.0 1.3 copy-start.1
  122.0 1.7 copy-start.2
  124.8 0.9 copy-start.5
  130.4 23.0 %all-to-all-start.3 = ((bf16[16,64,640]{2,1,0:T(8,128)(2,1)}), bf16[16,64,640]{2,1,0:T(8,128)(2,1)S(1)}, u32[]{:S(2)}, u32[]{:S(2)}) async-start(bf16[16,64,640]{2,1,0:T(8,128)(2,1)} %bitcast.27), calls=%async_computation.3 | async-start | bytes 2621440 | tf_op jit(solution)/shard_map/all_to_all | solution.py:13
  154.5 65.5 %copy-start.3 = (bf16[8,2560]{1,0:T(8,128)(2,1)S(1)}, bf16[8,2560]{1,0:T(8,128)(2,1)}, u32[]{:S(2)}) copy-start(bf16[8,2560]{1,0:T(8,128)(2,1)} %param.7) | copy-start | bytes 122884
  154.5 65.7 %copy-start.4 = (s32[8]{0:T(128)S(1)}, s32[8]{0:T(128)}, u32[]{:S(2)}) copy-start(s32[8]{0:T(128)} %param.8) | copy-start | bytes 100

commit v3 on v2

--- a/solution.py
+++ b/solution.py
@@ -1,3 +1,4 @@
+import itertools
 import math
 
 import jax
@@ -9,8 +10,23 @@
 CODE_COLUMNS = 128
 
 
-def exchange(buffer, axes):
-    return lax.all_to_all(buffer, axes, split_axis=0, concat_axis=0, tiled=True)
+AXES = ("x", "low", "core", "high", "row")
+
+
+def exchange(buffer, axes, groups=None):
+    return lax.all_to_all(buffer, axes, split_axis=0, concat_axis=0, axis_index_groups=groups, tiled=True)
+
+
+def window_groups():
+    n_x, n_low, n_core, n_high, n_row = (lax.axis_size(axis) for axis in AXES)
+    groups = []
+    for core, high, row in itertools.product(range(n_core), range(n_high), range(n_row)):
+        group = []
+        for x, low in itertools.product(range(n_x), range(n_low)):
+            run = (high + (core == 1 and low < n_low // 2)) % n_high
+            group.append((((x * n_low + low) * n_core + core) * n_high + run) * n_row + row)
+        groups.append(group)
+    return groups
 
 
 def swap_rows(rows, outer, inner, unit):
@@ -19,10 +35,14 @@
     return (source == lax.broadcasted_iota(jnp.int32, (rows, rows), 1)).astype(jnp.bfloat16)
 
 
+def reorder(matrix, rows):
+    return jnp.dot(matrix, rows, preferred_element_type=jnp.float32).astype(jnp.bfloat16)
+
+
 def shards(tokens, expert_ids, slot_ids, router, w_gate, w_up, hidden_grad):
-    n_high, n_row = lax.axis_size("high"), lax.axis_size("row")
-    n_x, n_pair = lax.axis_size("x"), lax.axis_size("pair")
-    n_tensor, n_expert = n_high * n_row, n_x * n_pair
+    n_x, n_low, n_core, n_high, n_row = (lax.axis_size(axis) for axis in AXES)
+    n_chip, n_tensor = n_x * n_low, n_high * n_row
+    n_expert = n_chip * n_core
     tok_rows, width = tokens.shape
     experts_all = router.shape[1]
     rows_all = hidden_grad.shape[1]
@@ -38,7 +58,7 @@
     token_float = tokens.astype(jnp.float32)
     routed_in = (router_score[:, None] * token_float).astype(jnp.bfloat16)
 
-    code = ((expert_ids % n_pair * n_x + expert_ids // n_pair) * capacity + slot_ids).astype(jnp.bfloat16)
+    code = (expert_ids * capacity + slot_ids).astype(jnp.bfloat16)
     pieces = routed_in.reshape(tok_rows, n_row, piece).transpose(1, 0, 2)
     codes = jnp.broadcast_to(code[None, :, None], (n_row, tok_rows, CODE_COLUMNS))
     outgoing = jnp.concatenate([pieces, codes], axis=2)
@@ -52,13 +72,14 @@
     slots = lax.dot_general(
         placed, group_rows[:, :piece], (((0,), (0,)), ((), ())), preferred_element_type=jnp.float32
     ).astype(jnp.bfloat16)
-    planes = exchange(slots.reshape(n_pair, n_x * capacity, piece), "pair").reshape(rows_all, piece)
-    x_first = swap_rows(rows_all, n_x, n_pair, capacity)
-    planes = jnp.dot(x_first, planes, preferred_element_type=jnp.float32).astype(jnp.bfloat16)
-    block = n_pair * capacity
-    planes = jnp.broadcast_to(planes.reshape(1, n_x, block, piece), (n_row, n_x, block, piece))
-    arrived = exchange(planes.reshape(n_row * n_x, block, piece), ("row", "x"))
-    arrived = arrived.reshape(n_row, rows_all, piece)
+    groups = window_groups()
+    core_first = swap_rows(rows_all, n_core, n_chip, capacity)
+    chip_first = swap_rows(rows_all, n_chip, n_core, capacity)
+    half = rows_all // n_core
+    chips = exchange(slots.reshape(n_chip, n_core * capacity, piece), AXES, groups)
+    chips = reorder(core_first, chips.reshape(rows_all, piece)).reshape(1, n_core, half, piece)
+    chips = jnp.broadcast_to(chips, (n_row, n_core, half, piece)).reshape(n_row * n_core, half, piece)
+    arrived = exchange(chips, ("row", "core")).reshape(n_row, rows_all, piece)
 
     gate_proj = jnp.zeros((rows_all, gate_weight.shape[1]), jnp.float32)
     lifted = gate_proj
@@ -69,8 +90,8 @@
     sigma_gate = jax.nn.sigmoid(gate_proj)
     silu_gate = gate_proj * sigma_gate
     silu_slope = sigma_gate * (1.0 + gate_proj * (1.0 - sigma_gate))
-    activation = (silu_gate * lifted).astype(jnp.bfloat16)
-    cotangent = hidden_grad[0].astype(jnp.float32)
+    activation = reorder(chip_first, (silu_gate * lifted).astype(jnp.bfloat16))
+    cotangent = reorder(core_first, hidden_grad[0]).astype(jnp.float32)
     d_gate = (cotangent * lifted * silu_slope).astype(jnp.bfloat16)
     d_lifted = (cotangent * silu_gate).astype(jnp.bfloat16)
     contract = (((1,), (1,)), ((), ()))
@@ -81,11 +102,10 @@
         part += lax.dot_general(d_lifted, up_weight[cut], contract, preferred_element_type=jnp.float32)
         partial.append(part.astype(jnp.bfloat16))
 
-    partial = exchange(jnp.stack(partial).reshape(n_row * n_x, block, piece), ("row", "x"))
+    partial = exchange(jnp.stack(partial).reshape(n_row * n_core, half, piece), ("row", "core"))
     summed = jnp.sum(partial.reshape(n_row, rows_all, piece).astype(jnp.float32), axis=0).astype(jnp.bfloat16)
-    pair_first = swap_rows(rows_all, n_pair, n_x, capacity)
-    summed = jnp.dot(pair_first, summed, preferred_element_type=jnp.float32).astype(jnp.bfloat16)
-    returned = exchange(summed.reshape(n_pair, n_x * capacity, piece), "pair").reshape(experts_all * capacity, piece)
+    summed = reorder(chip_first, summed).reshape(n_chip, n_core * capacity, piece)
+    returned = exchange(summed, AXES, groups).reshape(experts_all * capacity, piece)
     mine = jnp.dot(placed, returned, preferred_element_type=jnp.float32).astype(jnp.bfloat16)
     home = exchange(mine.reshape(n_tensor, tok_rows, piece), ("high", "row"))
     home = jnp.sum(home.reshape(n_high, n_row, tok_rows, piece).astype(jnp.float32), axis=0)
@@ -105,17 +125,16 @@
 def solution(mesh):
     n_expert, n_tensor = mesh.devices.shape
     n_row = n_x = math.isqrt(n_tensor)
-    axes = ("x", "pair", "high", "row")
-    split = Mesh(mesh.devices.reshape(n_x, n_expert // n_x, n_tensor // n_row, n_row), axes)
-    expert, tensor = axes[:2], axes[2:]
+    split = Mesh(mesh.devices.reshape(n_x, n_expert // (2 * n_x), 2, n_tensor // n_row, n_row), AXES)
+    expert, tensor = AXES[:3], AXES[3:]
     in_specs = (
-        P(axes, None),
-        P(axes),
-        P(axes),
+        P(AXES, None),
+        P(AXES),
+        P(AXES),
         P(),
         P(expert, None, tensor),
         P(expert, None, tensor),
         P(expert, None, tensor),
     )
-    out_specs = (P(expert, None, tensor), P(axes, None))
+    out_specs = (P(expert, None, tensor), P(AXES, None))
     return jax.shard_map(shards, mesh=split, in_specs=in_specs, out_specs=out_specs, check_vma=False)

time: 222 us -> 214 us (0.964)
  the two profiles are of different devices: /device:TPU:57 before, /device:TPU:34 now
where the time goes in v3:
time: 214 us
  blocking collectives  112 us (52%)
  waiting for transfers between devices  62.6 us (29%)
  starting transfers between devices  19.2 us (9%)
  matrix products  12.3 us (6%)
  other arithmetic  3.34 us (2%)
  local copies, waits for them, and re-layouts  2.95 us (1%)
    all_to_all x3, blocking collectives, exchange(): lax.all_to_all(buffer, axes, split_axis=0, concat_axis=0, axis_index_grou...  112 us
    all_to_all x3, waiting for transfers between devices, exchange(): lax.all_to_all(buffer, axes, split_axis=0, concat_axis=0, axis_index_grou...  62.6 us
    all_to_all x3, starting transfers between devices, exchange(): lax.all_to_all(buffer, axes, split_axis=0, concat_axis=0, axis_index_grou...  19.2 us
  transfers between devices with their start and end apart: 3, of which 3 were waited for; matrix products, arithmetic and copies ran while one was open for 1% of the time, Pallas kernels for 0%

profile of v3, /device:TPU:34, one launch (start us, length us, event | category | flops | bytes accessed | tf_op | source)
XLA Modules:
  0.0 213.8 jit_solution(2237766505745750236)
XLA Ops:
  0.6 0.0 copy-start
  0.6 1.0 copy-done
  1.6 1.1 fusion.15
  2.7 0.7 add_convert_fusion
  3.4 0.9 fusion.69
  4.3 0.1 broadcast_in_dim.15
  4.4 68.3 %all_to_all.30 = bf16[16,8,768]{2,1,0:T(8,128)(2,1)S(1)} all-to-all(bf16[16,8,768]{2,1,0:T(8,128)(2,1)S(1)} %bitcast.118), channel_id=1, replica_groups=mesh['x'=4,'low'=8,'core'=2,'high'=4,'row'=4] {'high','row'}, dimensions={0} | all-to-all | bytes 393216 | tf_op jit(solution)/shard_map/all_to_all | solution.py:17
  72.7 0.1 convert_reduce_fusion
  72.8 1.1 fusion.11
  73.9 8.4 %all-to-all-start.1 = ((bf16[32,8,640]{2,1,0:T(8,128)(2,1)}), bf16[32,8,640]{2,1,0:T(8,128)(2,1)S(1)}, u32[]{:S(2)}, u32[]{:S(2)}) async-start(bf16[32,8,640]{2,1,0:T(8,128)(2,1)} %fusion.11), calls=%async_computation.1 | async-start | bytes 655360 | tf_op jit(solution)/shard_map/all_to_all | solution.py:17
  82.3 13.9 %all-to-all-done.1 = bf16[32,8,640]{2,1,0:T(8,128)(2,1)S(1)} async-done(((bf16[32,8,640]{2,1,0:T(8,128)(2,1)}), bf16[32,8,640]{2,1,0:T(8,128)(2,1)S(1)}, u32[]{:S(2)}, u32[]{:S(2)}) %all-to-all-start.1) | async-done | bytes 327712 | tf_op jit(solution)/shard_map/all_to_all | solution.py:17
  96.2 0.9 convolution_convert_fusion.1
  97.1 0.1 broadcast_in_dim.18
  97.2 21.6 %all_to_all.31 = bf16[8,128,640]{2,1,0:T(8,128)(2,1)S(1)} all-to-all(bf16[8,128,640]{2,1,0:T(8,128)(2,1)S(1)} %bitcast.107), channel_id=1, replica_groups=mesh['x'=4,'low'=8,'core'=2,'high'=4,'row'=4] {'row','core'}, dimensions={0} | all-to-all | bytes 2621440 | tf_op jit(solution)/shard_map/all_to_all | solution.py:17
  118.8 0.0 copy-start.2
  118.8 0.0 copy-start.1
  118.8 0.1 fusion.84
  119.0 1.2 copy-done.2
  120.1 0.3 fusion.24
  120.4 0.1 copy-done.1
  120.5 0.3 fusion.37
  120.8 0.3 convolution_add_fusion.9
  121.1 0.3 convolution_add_fusion.6
  121.4 0.3 convolution_add_fusion.5
  121.6 0.3 convolution_add_fusion.8
  121.9 0.0 copy-start.5
  121.9 0.3 convolution_add_fusion.7
  122.2 0.3 convolution_add_fusion.4
  122.5 0.3 copy-done.5
  122.8 0.9 multiply_convert_fusion
  123.7 0.3 fusion.26
  124.0 0.3 fusion.29
  124.3 0.3 fusion.32
  124.6 0.3 fusion.35
  124.9 0.3 fusion.7
  125.2 0.3 fusion.8
  125.5 0.3 fusion.9
  125.8 0.3 fusion.10
  126.1 1.3 pad_maximum_fusion
  127.4 3.6 %all-to-all-start.3 = ((bf16[8,128,640]{2,1,0:T(8,128)(2,1)}), bf16[8,128,640]{2,1,0:T(8,128)(2,1)S(1)}, u32[]{:S(2)}, u32[]{:S(2)}) async-start(bf16[8,128,640]{2,1,0:T(8,128)(2,1)} %bitcast.26), calls=%async_computation.3 | async-start | bytes 2621440 | tf_op jit(solution)/shard_map/all_to_all | solution.py:17
  131.0 18.6 %all-to-all-done.3 = bf16[8,128,640]{2,1,0:T(8,128)(2,1)S(1)} async-done(((bf16[8,128,640]{2,1,0:T(8,128)(2,1)}), bf16[8,128,640]{2,1,0:T(8,128)(2,1)S(1)}, u32[]{:S(2)}, u32[]{:S(2)}) %all-to-all-start.3) | async-done | bytes 1310752 | tf_op jit(solution)/shard_map/all_to_all | solution.py:17
  149.6 0.2 bitcast_reduce_fusion
  149.8 0.9 fusion.6
  150.8 22.5 %all_to_all.32 = bf16[32,8,640]{2,1,0:T(8,128)(2,1)S(1)} all-to-all(bf16[32,8,640]{2,1,0:T(8,128)(2,1)S(1)} %fusion.6), channel_id=1, replica_groups={{0,32,64,96,128,160,192,224,256,288,320,352,384,416,448,480,512,544,576..., dimensions={0} | all-to-all | bytes 655360 | tf_op jit(solution)/shard_map/all_to_all | solution.py:17
  173.3 0.9 fusion.13
  174.2 7.3 %all-to-all-start.5 = ((bf16[16,8,640]{2,1,0:T(8,128)(2,1)}), bf16[16,8,640]{2,1,0:T(8,128)(2,1)S(1)}, u32[]{:S(2)}, u32[]{:S(2)}) async-start(bf16[16,8,640]{2,1,0:T(8,128)(2,1)} %fusion.13), calls=%async_computation.5 | async-start | bytes 327680 | tf_op jit(solution)/shard_map/all_to_all | solution.py:17
  181.5 0.0 copy-start.3
  181.5 0.0 copy-start.4
  181.5 1.2 fusion.14
  182.7 30.1 %all-to-all-done.5 = bf16[16,8,640]{2,1,0:T(8,128)(2,1)S(1)} async-done(((bf16[16,8,640]{2,1,0:T(8,128)(2,1)}), bf16[16,8,640]{2,1,0:T(8,128)(2,1)S(1)}, u32[]{:S(2)}, u32[]{:S(2)}) %all-to-all-start.5) | async-done | bytes 163872 | tf_op jit(solution)/shard_map/all_to_all | solution.py:17
  212.8 0.0 copy-done.3
  212.8 0.1 fusion.70
  212.9 0.0 copy-done.4
  212.9 0.8 fusion.1
  (13 shorter events, 0.1 us)
Async XLA Ops:
  0.6 1.0 copy-start
  73.9 22.3 %all-to-all-start.1 = ((bf16[32,8,640]{2,1,0:T(8,128)(2,1)}), bf16[32,8,640]{2,1,0:T(8,128)(2,1)S(1)}, u32[]{:S(2)}, u32[]{:S(2)}) async-start(bf16[32,8,640]{2,1,0:T(8,128)(2,1)} %fusion.11), calls=%async_computation.1 | async-start | bytes 655360 | tf_op jit(solution)/shard_map/all_to_all | solution.py:17
  118.8 1.3 copy-start.2
  118.8 1.7 copy-start.1
  121.9 0.9 copy-start.5
  127.4 22.2 %all-to-all-start.3 = ((bf16[8,128,640]{2,1,0:T(8,128)(2,1)}), bf16[8,128,640]{2,1,0:T(8,128)(2,1)S(1)}, u32[]{:S(2)}, u32[]{:S(2)}) async-start(bf16[8,128,640]{2,1,0:T(8,128)(2,1)} %bitcast.26), calls=%async_computation.3 | async-start | bytes 2621440 | tf_op jit(solution)/shard_map/all_to_all | solution.py:17
  174.2 38.5 %all-to-all-start.5 = ((bf16[16,8,640]{2,1,0:T(8,128)(2,1)}), bf16[16,8,640]{2,1,0:T(8,128)(2,1)S(1)}, u32[]{:S(2)}, u32[]{:S(2)}) async-start(bf16[16,8,640]{2,1,0:T(8,128)(2,1)} %fusion.13), calls=%async_computation.5 | async-start | bytes 327680 | tf_op jit(solution)/shard_map/all_to_all | solution.py:17
  181.5 31.3 %copy-start.3 = (bf16[8,2560]{1,0:T(8,128)(2,1)S(1)}, bf16[8,2560]{1,0:T(8,128)(2,1)}, u32[]{:S(2)}) copy-start(bf16[8,2560]{1,0:T(8,128)(2,1)} %param.7) | copy-start | bytes 122884
  181.5 31.4 %copy-start.4 = (s32[8]{0:T(128)S(1)}, s32[8]{0:T(128)}, u32[]{:S(2)}) copy-start(s32[8]{0:T(128)} %param.8) | copy-start | bytes 100

commit v4 on v3

v4 whole, which is shorter than its diff:
```python
import functools
import itertools
import math

import jax
import jax.numpy as jnp
from jax import lax
from jax.experimental import pallas as pl
from jax.experimental.pallas import tpu as pltpu
from jax.sharding import Mesh
from jax.sharding import PartitionSpec as P

CODE_COLUMNS = 128
WHOLE_VMEM = 66_500_000


AXES = ("x", "low", "core", "high", "row")


def exchange(buffer, axes, groups=None):
    return lax.all_to_all(buffer, axes, split_axis=0, concat_axis=0, axis_index_groups=groups, tiled=True)


def window_groups():
    n_x, n_low, n_core, n_high, n_row = (lax.axis_size(axis) for axis in AXES)
    groups = []
    for core, high, row in itertools.product(range(n_core), range(n_high), range(n_row)):
        group = []
        for x, low in itertools.product(range(n_x), range(n_low)):
            run = (high + (core == 1 and low < n_low // 2)) % n_high
            group.append((((x * n_low + low) * n_core + core) * n_high + run) * n_row + row)
        groups.append(group)
    return groups


def swap_rows(rows, outer, inner, unit):
    out = lax.broadcasted_iota(jnp.int32, (rows, rows), 0)
    source = (out // unit % inner * outer + out // (unit * inner)) * unit + out % unit
    return (source == lax.broadcasted_iota(jnp.int32, (rows, rows), 1)).astype(jnp.bfloat16)


def product(left, right, contract=(1, 0)):
    return lax.dot_general(
        left, right, (((contract[0],), (contract[1],)), ((), ())), preferred_element_type=jnp.float32
    )


def column(row):
    n = row.shape[1]
    diagonal = lax.broadcasted_iota(jnp.int32, (n, n), 0) == lax.broadcasted_iota(jnp.int32, (n, n), 1)
    values = jnp.broadcast_to(row.astype(jnp.float32), (n, n))
    return jnp.sum(jnp.where(diagonal, values, 0.0), axis=1, keepdims=True)


def send_kernel(n_row, capacity, *refs):
    sources, (out_ref, score_ref), buffers, sems = refs[:4], refs[4:6], refs[6:10], refs[10]
    copies = [pltpu.make_async_copy(sources[i], buffers[i], sems.at[i]) for i in range(4)]
    for copy in copies:
        copy.start()
    for copy in copies:
        copy.wait()
    tokens_ref, expert_ref, slot_ref, router_ref = buffers
    tok_rows, width = tokens_ref.shape
    piece = width // n_row
    experts = column(expert_ref[...])
    code = experts * capacity + column(slot_ref[...])
    logits = product(tokens_ref[...], router_ref[...], (1, 1))
    numbers = lax.broadcasted_iota(jnp.int32, logits.shape, 1).astype(jnp.float32)
    picked = jnp.sum(jnp.where(numbers == experts, logits, 0.0), axis=1, keepdims=True)
    score = jax.nn.sigmoid(picked)
    score_ref[...] = jnp.broadcast_to(score, score_ref.shape)
    codes = jnp.broadcast_to(code, (tok_rows, CODE_COLUMNS)).astype(jnp.bfloat16)
    for y in range(n_row):
        cut = pl.ds(y * piece, piece)
        scaled = (score * tokens_ref[:, cut].astype(jnp.float32)).astype(jnp.bfloat16)
        for high in range(out_ref.shape[0] // n_row):
            out_ref[high * n_row + y, :, pl.ds(0, piece)] = scaled
            out_ref[high * n_row + y, :, pl.ds(piece, CODE_COLUMNS)] = codes


def spread_kernel(order, rows_ref, out_ref):
    ordered = product(swap_rows(*order), rows_ref[...]).astype(jnp.bfloat16)
    for y in range(out_ref.shape[0]):
        out_ref[y] = ordered


def collect_kernel(order, parts_ref, out_ref):
    swap = swap_rows(*order)
    total = product(swap, parts_ref[0])
    for y in range(1, parts_ref.shape[0]):
        total += product(swap, parts_ref[y])
    out_ref[...] = total.astype(jnp.bfloat16)


def expert_kernel(order, back, rows_ref, hidden_ref, gate_ref, up_ref, act_ref, out_ref):
    n_row, _, piece = rows_ref.shape
    cuts = [pl.ds(y * piece, piece) for y in range(n_row)]
    cotangent = product(swap_rows(*order), hidden_ref[...])
    gate_proj = jnp.zeros(act_ref.shape, jnp.float32)
    lifted = gate_proj
    for y in range(n_row):
        gate_proj += product(rows_ref[y], gate_ref[cuts[y], :])
        lifted += product(rows_ref[y], up_ref[cuts[y], :])
    sigma_gate = jax.nn.sigmoid(gate_proj)
    silu_gate = gate_proj * sigma_gate
    silu_slope = sigma_gate * (1.0 + gate_proj * (1.0 - sigma_gate))
    activation = (silu_gate * lifted).astype(jnp.bfloat16)
    d_gate = (cotangent * lifted * silu_slope).astype(jnp.bfloat16)
    d_lifted = (cotangent * silu_gate).astype(jnp.bfloat16)
    for y in range(n_row):
        part = product(d_gate, gate_ref[cuts[y], :], (1, 1))
        part += product(d_lifted, up_ref[cuts[y], :], (1, 1))
        out_ref[y] = part.astype(jnp.bfloat16)
    act_ref[...] = product(swap_rows(*back), activation).astype(jnp.bfloat16)


VMEM_SPEC = pl.BlockSpec(memory_space=pltpu.VMEM)


def local_call(kernel, shape, inputs, flops, limit):
    moved = 2 * (math.prod(shape) + sum(value.size for value in inputs))
    return pl.pallas_call(
        kernel,
        out_shape=jax.ShapeDtypeStruct(shape, jnp.bfloat16),
        in_specs=[VMEM_SPEC] * len(inputs),
        out_specs=VMEM_SPEC,
        compiler_params=pltpu.CompilerParams(vmem_limit_bytes=limit),
        cost_estimate=pl.CostEstimate(flops=flops, bytes_accessed=moved, transcendentals=0),
    )(*inputs)


def run_expert(order, back, rows, hidden, gate_weight, up_weight):
    n_row, rows_all, piece = rows.shape
    width, units = gate_weight.shape
    return pl.pallas_call(
        functools.partial(expert_kernel, order, back),
        out_shape=(
            jax.ShapeDtypeStruct(hidden.shape, jnp.bfloat16),
            jax.ShapeDtypeStruct(rows.shape, jnp.bfloat16),
        ),
        in_specs=[VMEM_SPEC] * 4,
        out_specs=(VMEM_SPEC, VMEM_SPEC),
        compiler_params=pltpu.CompilerParams(vmem_limit_bytes=24 << 20),
        cost_estimate=pl.CostEstimate(
            flops=8 * rows_all * width * units, bytes_accessed=4 * width * units, transcendentals=rows_all * units
        ),
    )(rows, hidden, gate_weight, up_weight)


def shards(tokens, expert_ids, slot_ids, router, w_gate, w_up, hidden_grad):
    n_x, n_low, n_core, n_high, n_row = (lax.axis_size(axis) for axis in AXES)
    n_chip, n_tensor = n_x * n_low, n_high * n_row
    n_expert = n_chip * n_core
    tok_rows, width = tokens.shape
    experts_all = router.shape[1]
    rows_all = hidden_grad.shape[1]
    capacity = rows_all // n_expert
    piece = width // n_row
    group = n_tensor * tok_rows
    gate_weight, up_weight = w_gate[0], w_up[0]

    outgoing, scores = pl.pallas_call(
        functools.partial(send_kernel, n_row, capacity),
        out_shape=(
            jax.ShapeDtypeStruct((n_tensor, tok_rows, piece + CODE_COLUMNS), jnp.bfloat16),
            jax.ShapeDtypeStruct((tok_rows, CODE_COLUMNS), jnp.float32),
        ),
        in_specs=[pl.BlockSpec(memory_space=pltpu.HBM)] * 4,
        out_specs=(VMEM_SPEC, VMEM_SPEC),
        scratch_shapes=[
            pltpu.VMEM((tok_rows, width), jnp.bfloat16),
            pltpu.VMEM((1, tok_rows), jnp.int32),
            pltpu.VMEM((1, tok_rows), jnp.int32),
            pltpu.VMEM((experts_all, width), jnp.bfloat16),
            pltpu.SemaphoreType.DMA((4,)),
        ],
        compiler_params=pltpu.CompilerParams(vmem_limit_bytes=WHOLE_VMEM),
        cost_estimate=pl.CostEstimate(
            flops=2 * tok_rows * width * experts_all, bytes_accessed=2 * width * experts_all, transcendentals=tok_rows
        ),
    )(tokens, expert_ids.reshape(1, tok_rows), slot_ids.reshape(1, tok_rows), router.T)
    router_score = scores[:, 0]
    picked_mask = expert_ids[:, None] == jnp.arange(experts_all, dtype=jnp.int32)[None, :]
    token_float = tokens.astype(jnp.float32)
    group_rows = exchange(outgoing, ("high", "row")).reshape(group, piece + CODE_COLUMNS)

    slot_numbers = jnp.arange(experts_all * capacity, dtype=jnp.int32)
    placed = group_rows[:, piece : piece + 1].astype(jnp.int32) == slot_numbers[None, :]
    placed = placed.astype(jnp.bfloat16)
    slots = lax.dot_general(
        placed, group_rows[:, :piece], (((0,), (0,)), ((), ())), preferred_element_type=jnp.float32
    ).astype(jnp.bfloat16)
    groups = window_groups()
    core_first = (rows_all, n_core, n_chip, capacity)
    chip_first = (rows_all, n_chip, n_core, capacity)
    half = rows_all // n_core
    swap_flops = 2 * rows_all * rows_all * piece
    chips = exchange(slots.reshape(n_chip, n_core * capacity, piece), AXES, groups).reshape(rows_all, piece)
    chips = local_call(
        functools.partial(spread_kernel, core_first), (n_row, rows_all, piece), [chips], swap_flops, 8 << 20
    )
    arrived = exchange(chips.reshape(n_row * n_core, half, piece), ("row", "core"))

    activation, partial = run_expert(
        core_first, chip_first, arrived.reshape(n_row, rows_all, piece), hidden_grad[0], gate_weight, up_weight
    )

    partial = exchange(partial.reshape(n_row * n_core, half, piece), ("row", "core"))
    summed = local_call(
        functools.partial(collect_kernel, chip_first),
        (rows_all, piece),
        [partial.reshape(n_row, rows_all, piece)],
        n_row * swap_flops,
        8 << 20,
    )
    summed = summed.reshape(n_chip, n_core * capacity, piece)
    returned = exchange(summed, AXES, groups).reshape(experts_all * capacity, piece)
    mine = jnp.dot(placed, returned, preferred_element_type=jnp.float32).astype(jnp.bfloat16)
    home = exchange(mine.reshape(n_tensor, tok_rows, piece), ("high", "row"))
    home = jnp.sum(home.reshape(n_high, n_row, tok_rows, piece).astype(jnp.float32), axis=0)
    d_float = home.transpose(1, 0, 2).reshape(tok_rows, width).astype(jnp.bfloat16).astype(jnp.float32)

    inner = jnp.sum(token_float * d_float, axis=1)
    router_column = lax.dot_general(
        picked_mask.astype(jnp.bfloat16), router, (((1,), (1,)), ((), ())), preferred_element_type=jnp.float32
    )
    gradient = (
        router_score[:, None] * d_float
        + (inner * router_score * (1.0 - router_score))[:, None] * router_column
    )
    return activation[None], gradient.astype(jnp.bfloat16)


def solution(mesh):
    n_expert, n_tensor = mesh.devices.shape
    n_row = n_x = math.isqrt(n_tensor)
    split = Mesh(mesh.devices.reshape(n_x, n_expert // (2 * n_x), 2, n_tensor // n_row, n_row), AXES)
    expert, tensor = AXES[:3], AXES[3:]
    in_specs = (
        P(AXES, None),
        P(AXES),
        P(AXES),
        P(),
        P(expert, None, tensor),
        P(expert, None, tensor),
        P(expert, None, tensor),
    )
    out_specs = (P(expert, None, tensor), P(AXES, None))
    return jax.shard_map(shards, mesh=split, in_specs=in_specs, out_specs=out_specs, check_vma=False)
```

time: 214 us -> 203 us (0.949)
  blocking collectives: 112 us -> 195 us
  waiting for transfers between devices: 62.6 us -> 0 us
  starting transfers between devices: 19.2 us -> 0 us
  matrix products: 12.3 us -> 1.47 us
  Pallas kernels: 0 us -> 5.49 us
  other arithmetic: 3.34 us -> 0.33 us
  local copies, waits for them, and re-layouts: 2.95 us -> 0.2 us
    all_to_all x3 -> x6, blocking collectives: 112 us -> 195 us  [exchange(): lax.all_to_all(buffer, axes, split_axis=0, concat_axis=0, axis_index_grou...]
    all_to_all x3 -> x0, waiting for transfers between devices: 62.6 us -> none  [exchange(): lax.all_to_all(buffer, axes, split_axis=0, concat_axis=0, axis_index_grou...]
    all_to_all x3 -> x0, starting transfers between devices: 19.2 us -> none  [exchange(): lax.all_to_all(buffer, axes, split_axis=0, concat_axis=0, axis_index_grou...]
    dot_general x22 -> x1, matrix products: 10.3 us -> 0.84 us  [shards(): lax.dot_general(picked_mask.astype(jnp.bfloat16), router, (((1,), (1,)),...]
    pallas_call x0 -> x4, Pallas kernels: none -> 5.49 us  [the longest x1 2.61 us: run_expert(): pl.pallas_call(functools.partial(expert_kernel, order, back), out_shape=(...]
    unnamed x12 -> x15, local copies, waits for them, and re-layouts: 2.63 us -> 0.12 us
  transfers between devices with their start and end apart: 3 -> 0, of which waited for: 3 -> 0; matrix products, arithmetic and copies ran while one was open for 1% -> 0% of each run, Pallas kernels for 0% -> 0%
where the time goes in v4:
time: 203 us
  blocking collectives  195 us (96%)
  Pallas kernels  5.49 us (3%)
    all_to_all x6, blocking collectives, exchange(): lax.all_to_all(buffer, axes, split_axis=0, concat_axis=0, axis_index_grou...  195 us

profile of v4, /device:TPU:34, one launch (start us, length us, event | category | flops | bytes accessed | tf_op | source)
XLA Modules:
  0.0 203.0 jit_solution(6122351661629180762)
XLA Ops:
  0.6 2.0 %shard_map.86 = (bf16[16,8,768]{2,1,0:T(8,128)(2,1)}, f32[8,128]{1,0:T(8,128)}) custom-call(bf16[8,2560]{1,0:T(8,128)(2,1)} %refs_0_.1, s32[1,8]{1,0:T(1,128)} %bitcast.46, s32[1,8]{1,0:T(1,128)} %bitcast.47, bf16[64,2560]{1,0:T(8,128)(2,1)} %bitcast.39), custom_call_target="tpu_custom_call" | custom-call | flops 2621440 | bytes 327680 | tf_op jit(solution)/shard_map/pallas_call | solution.py:162
  2.7 68.5 %all_to_all.30 = bf16[16,8,768]{2,1,0:T(8,128)(2,1)S(1)} all-to-all(bf16[16,8,768]{2,1,0:T(8,128)(2,1)} %get-tuple-element.6), channel_id=1, replica_groups=mesh['x'=4,'low'=8,'core'=2,'high'=4,'row'=4] {'high','row'}, dimensions={0} | all-to-all | bytes 393216 | tf_op jit(solution)/shard_map/all_to_all | solution.py:21
  71.2 0.1 copy.13
  71.3 0.4 fusion.2
  71.7 22.1 %all_to_all.31 = bf16[32,8,640]{2,1,0:T(8,128)(2,1)S(1)} all-to-all(bf16[32,8,640]{2,1,0:T(8,128)(2,1)S(1)} %fusion.2), channel_id=1, replica_groups={{0,32,64,96,128,160,192,224,256,288,320,352,384,416,448,480,512,544,576..., dimensions={0} | all-to-all | bytes 655360 | tf_op jit(solution)/shard_map/all_to_all | solution.py:21
  93.8 0.0 copy-start.2
  93.8 0.3 shard_map.87
  94.1 0.0 copy-start
  94.1 0.0 copy-start.1
  94.1 21.7 %all_to_all.32 = bf16[8,128,640]{2,1,0:T(8,128)(2,1)S(1)} all-to-all(bf16[8,128,640]{2,1,0:T(8,128)(2,1)S(1)} %bitcast.30), channel_id=1, replica_groups=mesh['x'=4,'low'=8,'core'=2,'high'=4,'row'=4] {'row','core'}, dimensions={0} | all-to-all | bytes 2621440 | tf_op jit(solution)/shard_map/all_to_all | solution.py:21
  115.9 0.0 copy-done.2
  115.9 0.0 copy-done
  115.9 0.0 copy-done.1
  115.9 2.6 %shard_map.88 = (bf16[256,256]{1,0:T(8,128)(2,1)}, bf16[4,256,640]{2,1,0:T(8,128)(2,1)S(1)}) custom-call(bf16[4,256,640]{2,1,0:T(8,128)(2,1)S(1)} %bitcast.32, bf16[256,256]{1,0:T(8,128)(2,1)S(1)} %bitcast.38, bf16[2560,256]{1,0:T(8,128)(2,1)S(1)} %bitcast.36, bf16[2560,256]{1,0:T(8,128)(2,1)S(1)} %bitcast.37), custom_call_target="tpu_custom_call" | custom-call | flops 1342177280 | bytes 2621440 | tf_op jit(solution)/shard_map/pallas_call | solution.py:135
  118.5 21.2 %all_to_all.33 = bf16[8,128,640]{2,1,0:T(8,128)(2,1)S(1)} all-to-all(bf16[8,128,640]{2,1,0:T(8,128)(2,1)S(1)} %bitcast.33), channel_id=1, replica_groups=mesh['x'=4,'low'=8,'core'=2,'high'=4,'row'=4] {'row','core'}, dimensions={0} | all-to-all | bytes 2621440 | tf_op jit(solution)/shard_map/all_to_all | solution.py:21
  139.7 0.6 shard_map.89
  140.3 0.0 copy-start.4
  140.3 0.0 copy-start.5
  140.3 0.0 copy-start.3
  140.3 0.0 copy-start.6
  140.3 22.7 %all_to_all.34 = bf16[32,8,640]{2,1,0:T(8,128)(2,1)S(1)} all-to-all(bf16[32,8,640]{2,1,0:T(8,128)(2,1)S(1)} %bitcast.35), channel_id=1, replica_groups={{0,32,64,96,128,160,192,224,256,288,320,352,384,416,448,480,512,544,576..., dimensions={0} | all-to-all | bytes 655360 | tf_op jit(solution)/shard_map/all_to_all | solution.py:21
  163.0 0.2 fusion.3
  163.2 38.5 %all_to_all.35 = bf16[16,8,640]{2,1,0:T(8,128)(2,1)S(1)} all-to-all(bf16[16,8,640]{2,1,0:T(8,128)(2,1)S(1)} %fusion.3), channel_id=1, replica_groups=mesh['x'=4,'low'=8,'core'=2,'high'=4,'row'=4] {'high','row'}, dimensions={0} | all-to-all | bytes 327680 | tf_op jit(solution)/shard_map/all_to_all | solution.py:21
  201.7 0.0 copy-done.4
  201.7 0.1 multiply_reduce_fusion
  201.9 0.1 copy.12
  201.9 0.0 copy-done.5
  202.0 0.1 slice_reduce_fusion
  202.1 0.0 copy-done.3
  202.1 0.0 copy-done.6
  202.1 0.8 fusion.1
  (4 shorter events, 0.0 us)
Async XLA Ops:
  93.8 22.0 %copy-start.2 = (bf16[1,256,256]{2,1,0:T(8,128)(2,1)S(1)}, bf16[1,256,256]{2,1,0:T(8,128)(2,1)}, u32[]{:S(2)}) copy-start(bf16[1,256,256]{2,1,0:T(8,128)(2,1)} %param.13) | copy-start | bytes 393220
  94.1 21.8 %copy-start = (bf16[1,2560,256]{2,1,0:T(8,128)(2,1)S(1)}, bf16[1,2560,256]{2,1,0:T(8,128)(2,1)}, u32[]{:S(2)}) copy-start(bf16[1,2560,256]{2,1,0:T(8,128)(2,1)} %param.11) | copy-start | bytes 3932164
  94.1 21.7 %copy-start.1 = (bf16[1,2560,256]{2,1,0:T(8,128)(2,1)S(1)}, bf16[1,2560,256]{2,1,0:T(8,128)(2,1)}, u32[]{:S(2)}) copy-start(bf16[1,2560,256]{2,1,0:T(8,128)(2,1)} %param.12) | copy-start | bytes 3932164
  140.3 61.5 %copy-start.4 = (bf16[8,2560]{1,0:T(8,128)(2,1)S(1)}, bf16[8,2560]{1,0:T(8,128)(2,1)}, u32[]{:S(2)}) copy-start(bf16[8,2560]{1,0:T(8,128)(2,1)} %refs_0_.1) | copy-start | bytes 122884
  140.3 61.7 %copy-start.5 = (f32[8,128]{1,0:T(8,128)S(1)}, f32[8,128]{1,0:T(8,128)}, u32[]{:S(2)}) copy-start(f32[8,128]{1,0:T(8,128)} %get-tuple-element.8) | copy-start | bytes 12292
  140.3 61.8 %copy-start.3 = (bf16[2560,64]{0,1:T(8,128)(2,1)S(1)}, bf16[2560,64]{0,1:T(8,128)(2,1)}, u32[]{:S(2)}) copy-start(bf16[2560,64]{0,1:T(8,128)(2,1)} %param.10) | copy-start | bytes 983044
  140.3 61.8 %copy-start.6 = (s32[8]{0:T(128)S(1)}, s32[8]{0:T(128)}, u32[]{:S(2)}) copy-start(s32[8]{0:T(128)} %param.8) | copy-start | bytes 100

commit v5 on v4

--- a/solution.py
+++ b/solution.py
@@ -24,9 +24,9 @@
 def window_groups():
     n_x, n_low, n_core, n_high, n_row = (lax.axis_size(axis) for axis in AXES)
     groups = []
-    for core, high, row in itertools.product(range(n_core), range(n_high), range(n_row)):
+    for x, core, high, row in itertools.product(range(n_x), range(n_core), range(n_high), range(n_row)):
         group = []
-        for x, low in itertools.product(range(n_x), range(n_low)):
+        for low in range(n_low):
             run = (high + (core == 1 and low < n_low // 2)) % n_high
             group.append((((x * n_low + low) * n_core + core) * n_high + run) * n_row + row)
         groups.append(group)
@@ -35,7 +35,8 @@
 
 def swap_rows(rows, outer, inner, unit):
     out = lax.broadcasted_iota(jnp.int32, (rows, rows), 0)
-    source = (out // unit % inner * outer + out // (unit * inner)) * unit + out % unit
+    local = out % (outer * inner * unit)
+    source = out - local + (local // unit % inner * outer + local // (unit * inner)) * unit + local % unit
     return (source == lax.broadcasted_iota(jnp.int32, (rows, rows), 1)).astype(jnp.bfloat16)
 
 
@@ -52,7 +53,7 @@
     return jnp.sum(jnp.where(diagonal, values, 0.0), axis=1, keepdims=True)
 
 
-def send_kernel(n_row, capacity, *refs):
+def send_kernel(n_row, n_low, n_core, n_x, capacity, *refs):
     sources, (out_ref, score_ref), buffers, sems = refs[:4], refs[4:6], refs[6:10], refs[10]
     copies = [pltpu.make_async_copy(sources[i], buffers[i], sems.at[i]) for i in range(4)]
     for copy in copies:
@@ -62,8 +63,11 @@
     tokens_ref, expert_ref, slot_ref, router_ref = buffers
     tok_rows, width = tokens_ref.shape
     piece = width // n_row
-    experts = column(expert_ref[...])
-    code = experts * capacity + column(slot_ref[...])
+    expert = expert_ref[...]
+    chip, core = lax.div(expert, n_core), lax.rem(expert, n_core)
+    place = (lax.rem(chip, n_low) * n_x + lax.div(chip, n_low)) * n_core + core
+    experts = column(expert)
+    code = column(place * capacity + slot_ref[...])
     logits = product(tokens_ref[...], router_ref[...], (1, 1))
     numbers = lax.broadcasted_iota(jnp.int32, logits.shape, 1).astype(jnp.float32)
     picked = jnp.sum(jnp.where(numbers == experts, logits, 0.0), axis=1, keepdims=True)
@@ -149,8 +153,8 @@
 
 def shards(tokens, expert_ids, slot_ids, router, w_gate, w_up, hidden_grad):
     n_x, n_low, n_core, n_high, n_row = (lax.axis_size(axis) for axis in AXES)
-    n_chip, n_tensor = n_x * n_low, n_high * n_row
-    n_expert = n_chip * n_core
+    n_tensor = n_high * n_row
+    n_expert = n_x * n_low * n_core
     tok_rows, width = tokens.shape
     experts_all = router.shape[1]
     rows_all = hidden_grad.shape[1]
@@ -160,7 +164,7 @@
     gate_weight, up_weight = w_gate[0], w_up[0]
 
     outgoing, scores = pl.pallas_call(
-        functools.partial(send_kernel, n_row, capacity),
+        functools.partial(send_kernel, n_row, n_low, n_core, n_x, capacity),
         out_shape=(
             jax.ShapeDtypeStruct((n_tensor, tok_rows, piece + CODE_COLUMNS), jnp.bfloat16),
             jax.ShapeDtypeStruct((tok_rows, CODE_COLUMNS), jnp.float32),
@@ -191,29 +195,35 @@
         placed, group_rows[:, :piece], (((0,), (0,)), ((), ())), preferred_element_type=jnp.float32
     ).astype(jnp.bfloat16)
     groups = window_groups()
-    core_first = (rows_all, n_core, n_chip, capacity)
-    chip_first = (rows_all, n_chip, n_core, capacity)
-    half = rows_all // n_core
+    n_side = n_x * n_core
+    block = n_low * capacity
+    side_first = (rows_all, n_side, n_low, capacity)
+    low_first = (rows_all, n_low, n_side, capacity)
     swap_flops = 2 * rows_all * rows_all * piece
-    chips = exchange(slots.reshape(n_chip, n_core * capacity, piece), AXES, groups).reshape(rows_all, piece)
-    chips = local_call(
-        functools.partial(spread_kernel, core_first), (n_row, rows_all, piece), [chips], swap_flops, 8 << 20
-    )
-    arrived = exchange(chips.reshape(n_row * n_core, half, piece), ("row", "core"))
+    rows = exchange(slots.reshape(n_low, n_side * capacity, piece), AXES, groups).reshape(rows_all, piece)
+    rows = local_call(
+        functools.partial(spread_kernel, side_first), (n_row, rows_all, piece), [rows], swap_flops, 8 << 20
+    )
+    arrived = exchange(rows.reshape(n_row * n_side, block, piece), ("row", "x", "core"))
 
     activation, partial = run_expert(
-        core_first, chip_first, arrived.reshape(n_row, rows_all, piece), hidden_grad[0], gate_weight, up_weight
-    )
-
-    partial = exchange(partial.reshape(n_row * n_core, half, piece), ("row", "core"))
+        (rows_all, n_core, n_low, capacity),
+        (rows_all, n_low, n_core, capacity),
+        arrived.reshape(n_row, rows_all, piece),
+        hidden_grad[0],
+        gate_weight,
+        up_weight,
+    )
+
+    partial = exchange(partial.reshape(n_row * n_side, block, piece), ("row", "x", "core"))
     summed = local_call(
-        functools.partial(collect_kernel, chip_first),
+        functools.partial(collect_kernel, low_first),
         (rows_all, piece),
         [partial.reshape(n_row, rows_all, piece)],
         n_row * swap_flops,
         8 << 20,
     )
-    summed = summed.reshape(n_chip, n_core * capacity, piece)
+    summed = summed.reshape(n_low, n_side * capacity, piece)
     returned = exchange(summed, AXES, groups).reshape(experts_all * capacity, piece)
     mine = jnp.dot(placed, returned, preferred_element_type=jnp.float32).astype(jnp.bfloat16)
     home = exchange(mine.reshape(n_tensor, tok_rows, piece), ("high", "row"))

time: 203 us -> 207 us (1.020)
  the two profiles are of different devices: /device:TPU:34 before, /device:TPU:48 now
where the time goes in v5:
time: 207 us
  blocking collectives  198 us (96%)
  Pallas kernels  5.55 us (3%)
    all_to_all x6, blocking collectives, exchange(): lax.all_to_all(buffer, axes, split_axis=0, concat_axis=0, axis_index_grou...  198 us

profile of v5, /device:TPU:48, one launch (start us, length us, event | category | flops | bytes accessed | tf_op | source)
XLA Modules:
  0.0 206.8 jit_solution(9295868713981304370)
XLA Ops:
  0.6 2.0 shard_map.86
  2.7 67.2 %all_to_all.30 = bf16[16,8,768]{2,1,0:T(8,128)(2,1)S(1)} all-to-all(bf16[16,8,768]{2,1,0:T(8,128)(2,1)} %get-tuple-element.6), channel_id=1, replica_groups=mesh['x'=4,'low'=8,'core'=2,'high'=4,'row'=4] {'high','row'}, dimensions={0} | all-to-all | bytes 393216 | tf_op jit(solution)/shard_map/all_to_all | solution.py:21
  69.9 0.1 copy.13
  70.0 0.4 convolution_convert_fusion
  70.4 19.7 %all_to_all.31 = bf16[8,32,640]{2,1,0:T(8,128)(2,1)S(1)} all-to-all(bf16[8,32,640]{2,1,0:T(8,128)(2,1)S(1)} %bitcast.39), channel_id=1, replica_groups={{0,32,64,96,128,160,192,224},{1,33,65,97,129,161,193,225},{2,34,66,98,1..., dimensions={0} | all-to-all | bytes 655360 | tf_op jit(solution)/shard_map/all_to_all | solution.py:21
  90.1 0.0 copy-start.2
  90.1 0.3 shard_map.87
  90.4 0.0 copy-start
  90.4 0.0 copy-start.1
  90.4 25.2 %all_to_all.32 = bf16[32,32,640]{2,1,0:T(8,128)(2,1)S(1)} all-to-all(bf16[32,32,640]{2,1,0:T(8,128)(2,1)S(1)} %bitcast.28), channel_id=1, replica_groups=mesh['x'=4,'low'=8,'core'=2,'high'=4,'row'=4] {'row','x','core'}, dimensions={0} | all-to-all | bytes 2621440 | tf_op jit(solution)/shard_map/all_to_all | solution.py:21
  115.6 0.0 copy-done.2
  115.6 0.0 copy-done
  115.6 0.0 copy-done.1
  115.6 2.6 %shard_map.88 = (bf16[256,256]{1,0:T(8,128)(2,1)}, bf16[4,256,640]{2,1,0:T(8,128)(2,1)S(1)}) custom-call(bf16[4,256,640]{2,1,0:T(8,128)(2,1)S(1)} %bitcast.30, bf16[256,256]{1,0:T(8,128)(2,1)S(1)} %bitcast.36, bf16[2560,256]{1,0:T(8,128)(2,1)S(1)} %bitcast.34, bf16[2560,256]{1,0:T(8,128)(2,1)S(1)} %bitcast.35), custom_call_target="tpu_custom_call" | custom-call | flops 1342177280 | bytes 2621440 | tf_op jit(solution)/shard_map/pallas_call | solution.py:139
  118.3 23.7 %all_to_all.33 = bf16[32,32,640]{2,1,0:T(8,128)(2,1)S(1)} all-to-all(bf16[32,32,640]{2,1,0:T(8,128)(2,1)S(1)} %bitcast.31), channel_id=1, replica_groups=mesh['x'=4,'low'=8,'core'=2,'high'=4,'row'=4] {'row','x','core'}, dimensions={0} | all-to-all | bytes 2621440 | tf_op jit(solution)/shard_map/all_to_all | solution.py:21
  141.9 0.6 shard_map.89
  142.5 0.0 copy-start.4
  142.5 0.0 copy-start.5
  142.6 0.0 copy-start.3
  142.6 0.0 copy-start.6
  142.6 19.3 %all_to_all.34 = bf16[8,32,640]{2,1,0:T(8,128)(2,1)S(1)} all-to-all(bf16[8,32,640]{2,1,0:T(8,128)(2,1)S(1)} %bitcast.33), channel_id=1, replica_groups={{0,32,64,96,128,160,192,224},{1,33,65,97,129,161,193,225},{2,34,66,98,1..., dimensions={0} | all-to-all | bytes 655360 | tf_op jit(solution)/shard_map/all_to_all | solution.py:21
  161.9 0.2 fusion.2
  162.2 43.3 %all_to_all.35 = bf16[16,8,640]{2,1,0:T(8,128)(2,1)S(1)} all-to-all(bf16[16,8,640]{2,1,0:T(8,128)(2,1)S(1)} %fusion.2), channel_id=1, replica_groups=mesh['x'=4,'low'=8,'core'=2,'high'=4,'row'=4] {'high','row'}, dimensions={0} | all-to-all | bytes 327680 | tf_op jit(solution)/shard_map/all_to_all | solution.py:21
  205.5 0.0 copy-done.4
  205.6 0.1 multiply_reduce_fusion
  205.7 0.1 copy.12
  205.8 0.0 copy-done.5
  205.8 0.1 slice_reduce_fusion
  205.9 0.0 copy-done.3
  205.9 0.0 copy-done.6
  205.9 0.8 fusion.1
  (4 shorter events, 0.0 us)
Async XLA Ops:
  90.1 25.5 %copy-start.2 = (bf16[1,256,256]{2,1,0:T(8,128)(2,1)S(1)}, bf16[1,256,256]{2,1,0:T(8,128)(2,1)}, u32[]{:S(2)}) copy-start(bf16[1,256,256]{2,1,0:T(8,128)(2,1)} %param.13) | copy-start | bytes 393220
  90.4 25.2 %copy-start = (bf16[1,2560,256]{2,1,0:T(8,128)(2,1)S(1)}, bf16[1,2560,256]{2,1,0:T(8,128)(2,1)}, u32[]{:S(2)}) copy-start(bf16[1,2560,256]{2,1,0:T(8,128)(2,1)} %param.11) | copy-start | bytes 3932164
  90.4 25.2 %copy-start.1 = (bf16[1,2560,256]{2,1,0:T(8,128)(2,1)S(1)}, bf16[1,2560,256]{2,1,0:T(8,128)(2,1)}, u32[]{:S(2)}) copy-start(bf16[1,2560,256]{2,1,0:T(8,128)(2,1)} %param.12) | copy-start | bytes 3932164
  142.5 63.0 %copy-start.4 = (bf16[8,2560]{1,0:T(8,128)(2,1)S(1)}, bf16[8,2560]{1,0:T(8,128)(2,1)}, u32[]{:S(2)}) copy-start(bf16[8,2560]{1,0:T(8,128)(2,1)} %refs_0_.1) | copy-start | bytes 122884
  142.5 63.2 %copy-start.5 = (f32[8,128]{1,0:T(8,128)S(1)}, f32[8,128]{1,0:T(8,128)}, u32[]{:S(2)}) copy-start(f32[8,128]{1,0:T(8,128)} %get-tuple-element.8) | copy-start | bytes 12292
  142.6 63.4 %copy-start.3 = (bf16[2560,64]{0,1:T(8,128)(2,1)S(1)}, bf16[2560,64]{0,1:T(8,128)(2,1)}, u32[]{:S(2)}) copy-start(bf16[2560,64]{0,1:T(8,128)(2,1)} %param.10) | copy-start | bytes 983044
  142.6 63.4 %copy-start.6 = (s32[8]{0:T(128)S(1)}, s32[8]{0:T(128)}, u32[]{:S(2)}) copy-start(s32[8]{0:T(128)} %param.8) | copy-start | bytes 100

commit v6 on v4

--- a/solution.py
+++ b/solution.py
@@ -74,33 +74,43 @@
         cut = pl.ds(y * piece, piece)
         scaled = (score * tokens_ref[:, cut].astype(jnp.float32)).astype(jnp.bfloat16)
         for high in range(out_ref.shape[0] // n_row):
-            out_ref[high * n_row + y, :, pl.ds(0, piece)] = scaled
-            out_ref[high * n_row + y, :, pl.ds(piece, CODE_COLUMNS)] = codes
+            peer = y * (out_ref.shape[0] // n_row) + high
+            out_ref[peer, :, pl.ds(0, piece)] = scaled
+            out_ref[peer, :, pl.ds(piece, CODE_COLUMNS)] = codes
 
 
 def spread_kernel(order, rows_ref, out_ref):
     ordered = product(swap_rows(*order), rows_ref[...]).astype(jnp.bfloat16)
-    for y in range(out_ref.shape[0]):
-        out_ref[y] = ordered
+    peers, half, _ = out_ref.shape
+    n_row = peers * half // ordered.shape[0]
+    for peer in range(peers):
+        out_ref[peer] = ordered[peer // n_row * half : (peer // n_row + 1) * half]
+
+
+def all_cores(ref, n_row, y):
+    return jnp.concatenate([ref[peer] for peer in range(y, ref.shape[0], n_row)], axis=0)
 
 
 def collect_kernel(order, parts_ref, out_ref):
     swap = swap_rows(*order)
-    total = product(swap, parts_ref[0])
-    for y in range(1, parts_ref.shape[0]):
-        total += product(swap, parts_ref[y])
+    n_row = parts_ref.shape[0] * parts_ref.shape[1] // out_ref.shape[0]
+    total = product(swap, all_cores(parts_ref, n_row, 0))
+    for y in range(1, n_row):
+        total += product(swap, all_cores(parts_ref, n_row, y))
     out_ref[...] = total.astype(jnp.bfloat16)
 
 
 def expert_kernel(order, back, rows_ref, hidden_ref, gate_ref, up_ref, act_ref, out_ref):
-    n_row, _, piece = rows_ref.shape
+    peers, half, piece = rows_ref.shape
+    n_row = peers * half // hidden_ref.shape[0]
     cuts = [pl.ds(y * piece, piece) for y in range(n_row)]
     cotangent = product(swap_rows(*order), hidden_ref[...])
     gate_proj = jnp.zeros(act_ref.shape, jnp.float32)
     lifted = gate_proj
     for y in range(n_row):
-        gate_proj += product(rows_ref[y], gate_ref[cuts[y], :])
-        lifted += product(rows_ref[y], up_ref[cuts[y], :])
+        rows = all_cores(rows_ref, n_row, y)
+        gate_proj += product(rows, gate_ref[cuts[y], :])
+        lifted += product(rows, up_ref[cuts[y], :])
     sigma_gate = jax.nn.sigmoid(gate_proj)
     silu_gate = gate_proj * sigma_gate
     silu_slope = sigma_gate * (1.0 + gate_proj * (1.0 - sigma_gate))
@@ -110,7 +120,9 @@
     for y in range(n_row):
         part = product(d_gate, gate_ref[cuts[y], :], (1, 1))
         part += product(d_lifted, up_ref[cuts[y], :], (1, 1))
-        out_ref[y] = part.astype(jnp.bfloat16)
+        part = part.astype(jnp.bfloat16)
+        for core in range(peers // n_row):
+            out_ref[core * n_row + y] = part[core * half : (core + 1) * half]
     act_ref[...] = product(swap_rows(*back), activation).astype(jnp.bfloat16)
 
 
@@ -130,7 +142,7 @@
 
 
 def run_expert(order, back, rows, hidden, gate_weight, up_weight):
-    n_row, rows_all, piece = rows.shape
+    rows_all = hidden.shape[0]
     width, units = gate_weight.shape
     return pl.pallas_call(
         functools.partial(expert_kernel, order, back),
@@ -182,7 +194,7 @@
     router_score = scores[:, 0]
     picked_mask = expert_ids[:, None] == jnp.arange(experts_all, dtype=jnp.int32)[None, :]
     token_float = tokens.astype(jnp.float32)
-    group_rows = exchange(outgoing, ("high", "row")).reshape(group, piece + CODE_COLUMNS)
+    group_rows = exchange(outgoing, ("row", "high")).reshape(group, piece + CODE_COLUMNS)
 
     slot_numbers = jnp.arange(experts_all * capacity, dtype=jnp.int32)
     placed = group_rows[:, piece : piece + 1].astype(jnp.int32) == slot_numbers[None, :]
@@ -197,27 +209,27 @@
     swap_flops = 2 * rows_all * rows_all * piece
     chips = exchange(slots.reshape(n_chip, n_core * capacity, piece), AXES, groups).reshape(rows_all, piece)
     chips = local_call(
-        functools.partial(spread_kernel, core_first), (n_row, rows_all, piece), [chips], swap_flops, 8 << 20
-    )
-    arrived = exchange(chips.reshape(n_row * n_core, half, piece), ("row", "core"))
+        functools.partial(spread_kernel, core_first), (n_core * n_row, half, piece), [chips], swap_flops, 8 << 20
+    )
+    arrived = exchange(chips, ("core", "row"))
 
     activation, partial = run_expert(
-        core_first, chip_first, arrived.reshape(n_row, rows_all, piece), hidden_grad[0], gate_weight, up_weight
-    )
-
-    partial = exchange(partial.reshape(n_row * n_core, half, piece), ("row", "core"))
+        core_first, chip_first, arrived, hidden_grad[0], gate_weight, up_weight
+    )
+
+    partial = exchange(partial, ("core", "row"))
     summed = local_call(
         functools.partial(collect_kernel, chip_first),
         (rows_all, piece),
-        [partial.reshape(n_row, rows_all, piece)],
+        [partial],
         n_row * swap_flops,
         8 << 20,
     )
     summed = summed.reshape(n_chip, n_core * capacity, piece)
     returned = exchange(summed, AXES, groups).reshape(experts_all * capacity, piece)
     mine = jnp.dot(placed, returned, preferred_element_type=jnp.float32).astype(jnp.bfloat16)
-    home = exchange(mine.reshape(n_tensor, tok_rows, piece), ("high", "row"))
-    home = jnp.sum(home.reshape(n_high, n_row, tok_rows, piece).astype(jnp.float32), axis=0)
+    home = exchange(mine.reshape(n_tensor, tok_rows, piece), ("row", "high"))
+    home = jnp.sum(home.reshape(n_row, n_high, tok_rows, piece).astype(jnp.float32), axis=1)
     d_float = home.transpose(1, 0, 2).reshape(tok_rows, width).astype(jnp.bfloat16).astype(jnp.float32)
 
     inner = jnp.sum(token_float * d_float, axis=1)

time: 203 us -> 204 us (level)
  the two profiles are of different devices: /device:TPU:34 before, /device:TPU:32 now
where the time goes in v6:
time: 204 us; the launch traced here: 203 us
  blocking collectives  195 us (96%)
  Pallas kernels  5.49 us (3%)
    all_to_all x6, blocking collectives, exchange(): lax.all_to_all(buffer, axes, split_axis=0, concat_axis=0, axis_index_grou...  195 us

profile of v6, /device:TPU:32, one launch (start us, length us, event | category | flops | bytes accessed | tf_op | source)
XLA Modules:
  0.0 203.5 jit_solution(9554647108572412361)
XLA Ops:
  0.6 2.0 shard_map.86
  2.7 69.1 %all_to_all.30 = bf16[16,8,768]{2,1,0:T(8,128)(2,1)S(1)} all-to-all(bf16[16,8,768]{2,1,0:T(8,128)(2,1)} %get-tuple-element.6), channel_id=1, replica_groups=mesh['x'=4,'low'=8,'core'=2,'high'=4,'row'=4] {'row','high'}, dimensions={0} | all-to-all | bytes 393216 | tf_op jit(solution)/shard_map/all_to_all | solution.py:21
  71.8 0.1 copy.13
  71.9 0.4 fusion.2
  72.3 24.2 %all_to_all.31 = bf16[32,8,640]{2,1,0:T(8,128)(2,1)S(1)} all-to-all(bf16[32,8,640]{2,1,0:T(8,128)(2,1)S(1)} %fusion.2), channel_id=1, replica_groups={{0,32,64,96,128,160,192,224,256,288,320,352,384,416,448,480,512,544,576..., dimensions={0} | all-to-all | bytes 655360 | tf_op jit(solution)/shard_map/all_to_all | solution.py:21
  96.5 0.0 copy-start.2
  96.5 0.3 shard_map.87
  96.8 0.0 copy-start
  96.8 0.0 copy-start.1
  96.8 20.7 %all_to_all.32.rows_ref = bf16[8,128,640]{2,1,0:T(8,128)(2,1)S(1)} all-to-all(bf16[8,128,640]{2,1,0:T(8,128)(2,1)S(1)} %shard_map.87), channel_id=1, replica_groups=mesh['x'=4,'low'=8,'core'=2,'high'=4,'row'=4] {'core','row'}, dimensions={0} | all-to-all | bytes 2621440 | tf_op jit(solution)/shard_map/all_to_all | solution.py:21
  117.5 0.0 copy-done.2
  117.5 0.0 copy-done
  117.5 0.0 copy-done.1
  117.5 2.6 %shard_map.88 = (bf16[256,256]{1,0:T(8,128)(2,1)}, bf16[8,128,640]{2,1,0:T(8,128)(2,1)S(1)}) custom-call(bf16[8,128,640]{2,1,0:T(8,128)(2,1)S(1)} %all_to_all.32.rows_ref, bf16[256,256]{1,0:T(8,128)(2,1)S(1)} %bitcast.31, bf16[2560,256]{1,0:T(8,128)(2,1)S(1)} %bitcast.29, bf16[2560,256]{1,0:T(8,128)(2,1)S(1)} %bitcast.30), custom_call_target="tpu_custom_call" | custom-call | flops 1342177280 | bytes 2621440 | tf_op jit(solution)/shard_map/pallas_call | solution.py:147
  120.1 21.0 %all_to_all.33.parts_ref = bf16[8,128,640]{2,1,0:T(8,128)(2,1)S(1)} all-to-all(bf16[8,128,640]{2,1,0:T(8,128)(2,1)S(1)} %get-tuple-element.9), channel_id=1, replica_groups=mesh['x'=4,'low'=8,'core'=2,'high'=4,'row'=4] {'core','row'}, dimensions={0} | all-to-all | bytes 2621440 | tf_op jit(solution)/shard_map/all_to_all | solution.py:21
  141.1 0.6 shard_map.89
  141.7 0.0 copy-start.4
  141.7 0.0 copy-start.5
  141.7 0.0 copy-start.3
  141.7 0.0 copy-start.6
  141.7 22.7 %all_to_all.34 = bf16[32,8,640]{2,1,0:T(8,128)(2,1)S(1)} all-to-all(bf16[32,8,640]{2,1,0:T(8,128)(2,1)S(1)} %bitcast.28), channel_id=1, replica_groups={{0,32,64,96,128,160,192,224,256,288,320,352,384,416,448,480,512,544,576..., dimensions={0} | all-to-all | bytes 655360 | tf_op jit(solution)/shard_map/all_to_all | solution.py:21
  164.4 0.2 fusion.3
  164.6 37.5 %all_to_all.35 = bf16[16,8,640]{2,1,0:T(8,128)(2,1)S(1)} all-to-all(bf16[16,8,640]{2,1,0:T(8,128)(2,1)S(1)} %fusion.3), channel_id=1, replica_groups=mesh['x'=4,'low'=8,'core'=2,'high'=4,'row'=4] {'row','high'}, dimensions={0} | all-to-all | bytes 327680 | tf_op jit(solution)/shard_map/all_to_all | solution.py:21
  202.2 0.0 copy-done.4
  202.2 0.1 multiply_reduce_fusion
  202.4 0.1 copy.12
  202.4 0.0 copy-done.5
  202.4 0.1 slice_reduce_fusion
  202.6 0.0 copy-done.3
  202.6 0.0 copy-done.6
  202.6 0.8 fusion.1
  (4 shorter events, 0.0 us)
Async XLA Ops:
  96.5 21.0 %copy-start.2 = (bf16[1,256,256]{2,1,0:T(8,128)(2,1)S(1)}, bf16[1,256,256]{2,1,0:T(8,128)(2,1)}, u32[]{:S(2)}) copy-start(bf16[1,256,256]{2,1,0:T(8,128)(2,1)} %param.13) | copy-start | bytes 393220
  96.8 20.7 %copy-start = (bf16[1,2560,256]{2,1,0:T(8,128)(2,1)S(1)}, bf16[1,2560,256]{2,1,0:T(8,128)(2,1)}, u32[]{:S(2)}) copy-start(bf16[1,2560,256]{2,1,0:T(8,128)(2,1)} %param.11) | copy-start | bytes 3932164
  96.8 20.7 %copy-start.1 = (bf16[1,2560,256]{2,1,0:T(8,128)(2,1)S(1)}, bf16[1,2560,256]{2,1,0:T(8,128)(2,1)}, u32[]{:S(2)}) copy-start(bf16[1,2560,256]{2,1,0:T(8,128)(2,1)} %param.12) | copy-start | bytes 3932164
  141.7 60.6 %copy-start.4 = (bf16[8,2560]{1,0:T(8,128)(2,1)S(1)}, bf16[8,2560]{1,0:T(8,128)(2,1)}, u32[]{:S(2)}) copy-start(bf16[8,2560]{1,0:T(8,128)(2,1)} %refs_0_.1) | copy-start | bytes 122884
  141.7 60.8 %copy-start.5 = (f32[8,128]{1,0:T(8,128)S(1)}, f32[8,128]{1,0:T(8,128)}, u32[]{:S(2)}) copy-start(f32[8,128]{1,0:T(8,128)} %get-tuple-element.8) | copy-start | bytes 12292
  141.7 60.9 %copy-start.3 = (bf16[2560,64]{0,1:T(8,128)(2,1)S(1)}, bf16[2560,64]{0,1:T(8,128)(2,1)}, u32[]{:S(2)}) copy-start(bf16[2560,64]{0,1:T(8,128)(2,1)} %param.10) | copy-start | bytes 983044
  141.7 60.9 %copy-start.6 = (s32[8]{0:T(128)S(1)}, s32[8]{0:T(128)}, u32[]{:S(2)}) copy-start(s32[8]{0:T(128)} %param.8) | copy-start | bytes 100
